TPU v7x, 32 devices: a whole 2x2x4 slice. The times are simulated.
32 devices in a mesh: dp: 16 (over z, x, core), tensor: 2 (over y).
Axes of the slice: x: 2, y: 2, z: 4, core: 2. Of those that a mesh axis runs over, the one named last changes fastest.
Arguments:
- layer_input: bfloat16 [16384, 768], P(('dp', 'tensor')), may hold values from -11 to 11
- grad_out: bfloat16 [16384, 768], P(('dp', 'tensor')), may hold values from -6 to 6
- segment: int32 [16384], P('dp'), may hold values from 0 to 63, never falling along the last dimension, each value on 1 to 1024 neighbouring positions
- entity: int32 [16384], P('dp'), may hold values 0 or 1
- valid_mask: int32 [16384], P('dp'), may hold values from 0 to 1, as said below
- query_weight: bfloat16 [4, 768, 768], P(None, 'dp', 'tensor'), may hold values from -0.4375 to 0.4375
- key_value_weight: bfloat16 [2, 768, 768], P(None, 'dp', 'tensor'), may hold values from -0.21875 to 0.21875
- attn_bias: bfloat16 [5, 768], P(None, 'tensor'), may hold values from -3 to 3
- out_weight: bfloat16 [768, 768], P('tensor', 'dp'), may hold values from -0.875 to 0.875
- out_bias: bfloat16 [2, 768], replicated, may hold values from -2 to 2
- ln_gain: bfloat16 [2, 768], replicated, may hold values from 0.25 to 1.75
- ln_bias: bfloat16 [2, 768], replicated, may hold values from -2 to 2
- up_weight: bfloat16 [768, 3072], P('dp', 'tensor'), may hold values from -0.21875 to 0.21875
- ffn_bias: bfloat16 [3072], P('tensor'), may hold values from -3 to 3
- down_weight: bfloat16 [3072, 768], P('tensor', 'dp'), may hold values from -0.109375 to 0.109375
Outputs:
- output: bfloat16 [16384, 768], P(('dp', 'tensor'))
- input_grad: float32 [16384, 768], P(('dp', 'tensor'))
- residual_rms: float32 [4], replicated
- query_weight_grad: float32 [4, 768, 768], P(None, 'dp', 'tensor')
- key_value_weight_grad: float32 [2, 768, 768], P(None, 'dp', 'tensor')
- attn_bias_grad: float32 [5, 768], P(None, 'tensor')
- out_weight_grad: float32 [768, 768], P('tensor', 'dp')
- out_bias_grad: float32 [2, 768], replicated
- ln_gain_grad: float32 [2, 768], replicated
- ln_bias_grad: float32 [2, 768], replicated
- up_weight_grad: float32 [768, 3072], P('dp', 'tensor')
- ffn_bias_grad: float32 [3072], P('tensor')
- down_weight_grad: float32 [3072, 768], P('tensor', 'dp')
Inputs may be any that keep to these rules, and one draw needn't show every extreme that they name: segment numbers never fall along the tokens. `valid_mask`: the first token of every sequence of 1024 tokens is real.
All inputs are finite; a program needn't handle non-finite values. No bound on the sum of `entity` on one device may be relied on, other than what follows from the above.
Results may differ from a plain program's by a relative error of at most 0.017.
Values may be sent and summed in bfloat16 or wider, within the bound.
A program may use at most 128 MiB of HBM per device.

v0:
```python
import jax
import jax.numpy as jnp
from jax import lax
from jax.sharding import PartitionSpec as P

HEAD = 64


EPS = 1e-06
NEG = -1e30


def layer_norm(resid, gain, shift):
    center = resid - jnp.mean(resid, -1, keepdims=True)
    spread = jnp.mean(center * center, -1, keepdims=True)
    return center * lax.rsqrt(spread + EPS) * gain + shift


def gelu_exact(values):
    return jax.nn.gelu(values, approximate=False)


def to_blocks(array_in, blocks):
    return array_in.reshape((blocks, array_in.shape[0] // blocks) + array_in.shape[1:])


def fetch_weights(query_weight, key_value_weight, out_weight, up_weight, down_weight):
    return (
        lax.all_gather(query_weight, "dp", axis=1, tiled=True),
        lax.all_gather(key_value_weight, "dp", axis=1, tiled=True),
        lax.all_gather(out_weight, "dp", axis=1, tiled=True),
        lax.all_gather(up_weight, "dp", axis=0, tiled=True),
        lax.all_gather(down_weight, "dp", axis=1, tiled=True),
    )


def block_scores(
    word_block,
    ent_block,
    seg_block,
    pos_block,
    keys3,
    seg_keys,
    ent_keys,
    valid_keys,
    key_pos,
    scale,
):
    score_word = jnp.einsum("qhd,khd->hqk", word_block, keys3, preferred_element_type=jnp.float32)
    score_ent = jnp.einsum("qhd,khd->hqk", ent_block, keys3, preferred_element_type=jnp.float32)
    scores = jnp.where(ent_keys[None, None, :], score_ent, score_word) * scale
    allowed = (seg_block[:, None] == seg_keys[None, :]) & (
        valid_keys[None, :] | (pos_block[:, None] == key_pos[None, :])
    )
    return jnp.where(allowed[None], scores, NEG)


def body(
    layer_input,
    grad_out,
    segment,
    entity,
    valid_mask,
    query_weight,
    key_value_weight,
    attn_bias,
    out_weight,
    out_bias,
    ln_gain,
    ln_bias,
    up_weight,
    ffn_bias,
    down_weight,
):
    rows = layer_input.shape[0]
    width = layer_input.shape[1]
    tensor_rank = lax.axis_index("tensor")
    tensor_count = lax.axis_size("tensor")
    length = segment.shape[0]
    cols = query_weight.shape[2]
    heads_here = cols // HEAD
    half_ff = ffn_bias.shape[0]
    scale = HEAD ** (-0.5)
    block = min(512, length)
    blocks = length // block
    own_start = tensor_rank * rows
    ent_flag = entity == 1
    valid_flag = valid_mask == 1
    positions = jnp.arange(length, dtype=jnp.int32)
    shape3 = (length, heads_here, HEAD)
    query_full, kv_full, out_full, up_full, down_full = fetch_weights(
        query_weight, key_value_weight, out_weight, up_weight, down_weight
    )
    tokens_all = lax.all_gather(layer_input, "tensor", axis=0, tiled=True)
    query_four = jnp.einsum(
        "ld,mde->mle", tokens_all, query_full, preferred_element_type=jnp.float32
    )
    query_four = query_four + attn_bias[:4, None, :].astype(jnp.float32)
    ent_col = ent_flag[:, None]
    query_word = jnp.where(ent_col, query_four[2], query_four[0]).astype(jnp.bfloat16)
    query_ent = jnp.where(ent_col, query_four[3], query_four[1]).astype(jnp.bfloat16)
    key_value = jnp.einsum("ld,mde->mle", tokens_all, kv_full, preferred_element_type=jnp.float32)
    keys3 = key_value[0].astype(jnp.bfloat16).reshape(shape3)
    values3 = (key_value[1] + attn_bias[4].astype(jnp.float32)).astype(jnp.bfloat16).reshape(shape3)
    word_blocks = to_blocks(query_word.reshape(shape3), blocks)
    ent_blocks = to_blocks(query_ent.reshape(shape3), blocks)
    seg_blocks = to_blocks(segment, blocks)
    pos_blocks = to_blocks(positions, blocks)

    def forward_block(pieces):
        word_block, ent_block, seg_block, pos_block = pieces
        masked = block_scores(
            word_block,
            ent_block,
            seg_block,
            pos_block,
            keys3,
            segment,
            ent_flag,
            valid_flag,
            positions,
            scale,
        )
        row_max = jnp.max(masked, -1, keepdims=True)
        expo_vals = jnp.exp(masked - row_max)
        totals = jnp.sum(expo_vals, -1, keepdims=True)
        probs = expo_vals / totals
        context = jnp.einsum(
            "hqk,khd->qhd", probs.astype(jnp.bfloat16), values3, preferred_element_type=jnp.float32
        )
        return (
            context.reshape(block, cols).astype(jnp.bfloat16),
            (row_max + jnp.log(totals))[..., 0],
        )

    context_blocks, lse_blocks = lax.map(
        forward_block, (word_blocks, ent_blocks, seg_blocks, pos_blocks)
    )
    context_all = context_blocks.reshape(length, cols)
    attn = lax.psum_scatter(
        jnp.dot(context_all, out_full, preferred_element_type=jnp.float32).astype(jnp.bfloat16),
        "tensor",
        scatter_dimension=0,
        tiled=True,
    ).astype(jnp.float32) + out_bias[0].astype(jnp.float32)
    resid_one = layer_input.astype(jnp.float32) + attn
    hidden, ln_one_pull = jax.vjp(
        layer_norm, resid_one, ln_gain[0].astype(jnp.float32), ln_bias[0].astype(jnp.float32)
    )
    hidden_low = hidden.astype(jnp.bfloat16)
    ffn_rows = lax.all_gather(hidden_low, "tensor", axis=0, tiled=True)
    pre = jnp.dot(ffn_rows, up_full, preferred_element_type=jnp.float32) + ffn_bias.astype(
        jnp.float32
    )
    active, gelu_pull = jax.vjp(gelu_exact, pre)
    active_low = active.astype(jnp.bfloat16)
    ffn = lax.psum_scatter(
        jnp.dot(active_low, down_full, preferred_element_type=jnp.float32).astype(jnp.bfloat16),
        "tensor",
        scatter_dimension=0,
        tiled=True,
    ).astype(jnp.float32) + out_bias[1].astype(jnp.float32)
    resid_two = hidden + ffn
    result, ln_two_pull = jax.vjp(
        layer_norm, resid_two, ln_gain[1].astype(jnp.float32), ln_bias[1].astype(jnp.float32)
    )
    output = result.astype(jnp.bfloat16)
    valid_own = lax.dynamic_slice_in_dim(valid_mask, own_start, rows).astype(jnp.float32)[:, None]
    stat_terms = jnp.stack(
        [
            jnp.sum(valid_own * resid_one * resid_one),
            jnp.sum(valid_own * attn * attn),
            jnp.sum(valid_own * ffn * ffn),
            jnp.sum(valid_own * resid_two * resid_two),
            jnp.sum(valid_own),
        ]
    )
    query_full, kv_full, out_full, up_full, down_full = fetch_weights(
        query_weight, key_value_weight, out_weight, up_weight, down_weight
    )
    d_two, gain_two, shift_two = ln_two_pull(grad_out.astype(jnp.float32))
    d_ffn = d_two.astype(jnp.bfloat16)
    bias_two = jnp.sum(d_ffn.astype(jnp.float32), 0)
    ffn_grad_rows = lax.all_gather(d_ffn, "tensor", axis=0, tiled=True)
    d_active = jnp.einsum("ld,fd->lf", ffn_grad_rows, down_full, preferred_element_type=jnp.float32)
    (d_pre,) = gelu_pull(d_active)
    d_pre_low = d_pre.astype(jnp.bfloat16)
    down_grad = jnp.einsum(
        "lf,ld->fd", active_low, ffn_grad_rows, preferred_element_type=jnp.float32
    )
    up_grad = jnp.einsum("ld,lf->df", ffn_rows, d_pre_low, preferred_element_type=jnp.float32)
    bias_ffn_grad = jnp.sum(d_pre_low.astype(jnp.float32), 0)
    d_hidden = d_two + lax.psum_scatter(
        jnp.einsum("lf,df->ld", d_pre_low, up_full, preferred_element_type=jnp.float32).astype(
            jnp.bfloat16
        ),
        "tensor",
        scatter_dimension=0,
        tiled=True,
    ).astype(jnp.float32)
    ffn_bias_full = lax.dynamic_update_slice_in_dim(
        jnp.zeros((half_ff * tensor_count,), jnp.float32), bias_ffn_grad, tensor_rank * half_ff, 0
    )
    d_one, gain_one, shift_one = ln_one_pull(d_hidden)
    d_attn = d_one.astype(jnp.bfloat16)
    bias_one = jnp.sum(d_attn.astype(jnp.float32), 0)
    attn_grad_rows = lax.all_gather(d_attn, "tensor", axis=0, tiled=True)
    d_context = jnp.einsum(
        "ld,cd->lc", attn_grad_rows, out_full, preferred_element_type=jnp.float32
    ).astype(jnp.bfloat16)
    out_grad = jnp.einsum(
        "lc,ld->cd", context_all, attn_grad_rows, preferred_element_type=jnp.float32
    )

    def backward_block(carry, pieces):
        key_acc, value_acc = carry
        word_block, ent_block, seg_block, pos_block, lse_block, dctx_block = pieces
        masked = block_scores(
            word_block,
            ent_block,
            seg_block,
            pos_block,
            keys3,
            segment,
            ent_flag,
            valid_flag,
            positions,
            scale,
        )
        probs = jnp.exp(masked - lse_block[..., None])
        d_probs = jnp.einsum(
            "qhd,khd->hqk", dctx_block, values3, preferred_element_type=jnp.float32
        )
        delta = jnp.sum(probs * d_probs, -1, keepdims=True)
        d_scores = (probs * (d_probs - delta)).astype(jnp.bfloat16)
        zero_low = jnp.zeros_like(d_scores)
        ent_keys3 = ent_flag[None, None, :]
        d_word = jnp.where(ent_keys3, zero_low, d_scores)
        d_ent = jnp.where(ent_keys3, d_scores, zero_low)
        grad_word = (
            jnp.einsum("hqk,khd->qhd", d_word, keys3, preferred_element_type=jnp.float32) * scale
        )
        grad_ent = (
            jnp.einsum("hqk,khd->qhd", d_ent, keys3, preferred_element_type=jnp.float32) * scale
        )
        key_term = jnp.einsum(
            "hqk,qhd->khd", d_word, word_block, preferred_element_type=jnp.float32
        )
        key_term = key_term + jnp.einsum(
            "hqk,qhd->khd", d_ent, ent_block, preferred_element_type=jnp.float32
        )
        key_acc = key_acc + key_term * scale
        value_acc = value_acc + jnp.einsum(
            "hqk,qhd->khd",
            probs.astype(jnp.bfloat16),
            dctx_block,
            preferred_element_type=jnp.float32,
        )
        return (
            (key_acc, value_acc),
            (grad_word.reshape(block, cols), grad_ent.reshape(block, cols)),
        )

    zero3 = jnp.zeros(shape3, jnp.float32)
    dctx_blocks = to_blocks(d_context.reshape(shape3), blocks)
    (key_acc, value_acc), (word_grads, ent_grads) = lax.scan(
        backward_block,
        (zero3, zero3),
        (word_blocks, ent_blocks, seg_blocks, pos_blocks, lse_blocks, dctx_blocks),
    )
    d_word_q = word_grads.reshape(length, cols).astype(jnp.bfloat16)
    d_ent_q = ent_grads.reshape(length, cols).astype(jnp.bfloat16)
    d_keys = key_acc.reshape(length, cols).astype(jnp.bfloat16)
    d_values = value_acc.reshape(length, cols).astype(jnp.bfloat16)
    zero_rows = jnp.zeros_like(d_word_q)
    d_queries = jnp.stack(
        [
            jnp.where(ent_col, zero_rows, d_word_q),
            jnp.where(ent_col, zero_rows, d_ent_q),
            jnp.where(ent_col, d_word_q, zero_rows),
            jnp.where(ent_col, d_ent_q, zero_rows),
        ]
    )
    d_kv = jnp.stack([d_keys, d_values])
    query_grad = jnp.einsum(
        "ld,mle->mde", tokens_all, d_queries, preferred_element_type=jnp.float32
    )
    kv_grad = jnp.einsum("ld,mle->mde", tokens_all, d_kv, preferred_element_type=jnp.float32)
    attn_bias_part = jnp.concatenate(
        [jnp.sum(d_queries.astype(jnp.float32), 1), jnp.sum(d_values.astype(jnp.float32), 0)[None]],
        0,
    )
    total = jnp.einsum("mle,mde->ld", d_queries, query_full, preferred_element_type=jnp.float32)
    input_grad = d_one + lax.psum_scatter(
        (
            total + jnp.einsum("mle,mde->ld", d_kv, kv_full, preferred_element_type=jnp.float32)
        ).astype(jnp.bfloat16),
        "tensor",
        scatter_dimension=0,
        tiled=True,
    ).astype(jnp.float32)
    query_shard, kv_shard, out_shard, up_shard, down_shard = (
        lax.psum_scatter(query_grad, "dp", scatter_dimension=1, tiled=True),
        lax.psum_scatter(kv_grad, "dp", scatter_dimension=1, tiled=True),
        lax.psum_scatter(out_grad, "dp", scatter_dimension=1, tiled=True),
        lax.psum_scatter(up_grad, "dp", scatter_dimension=0, tiled=True),
        lax.psum_scatter(down_grad, "dp", scatter_dimension=1, tiled=True),
    )
    attn_bias_full = lax.dynamic_update_slice_in_dim(
        jnp.zeros((5, cols * tensor_count), jnp.float32), attn_bias_part, tensor_rank * cols, 1
    )
    summed = lax.psum(
        (
            jnp.stack([gain_one, gain_two]),
            jnp.stack([shift_one, shift_two]),
            jnp.stack([bias_one, bias_two]),
            attn_bias_full,
            ffn_bias_full,
            stat_terms,
        ),
        ("dp", "tensor"),
    )
    gains_sum, shifts_sum, out_bias_sum, attn_bias_sum, ffn_bias_sum, stat_sum = summed
    attn_bias_grad = lax.dynamic_slice_in_dim(attn_bias_sum, tensor_rank * cols, cols, 1)
    ffn_bias_grad = lax.dynamic_slice_in_dim(ffn_bias_sum, tensor_rank * half_ff, half_ff, 0)
    residual_rms = jnp.sqrt(stat_sum[:4] / (stat_sum[4] * width))
    return (
        output,
        input_grad,
        residual_rms,
        query_shard,
        kv_shard,
        attn_bias_grad,
        out_shard,
        out_bias_sum,
        gains_sum,
        shifts_sum,
        up_shard,
        ffn_bias_grad,
        down_shard,
    )


def solution(mesh):
    placed = (
        P(("dp", "tensor"), None),
        P(("dp", "tensor"), None),
        P("dp"),
        P("dp"),
        P("dp"),
        P(None, "dp", "tensor"),
        P(None, "dp", "tensor"),
        P(None, "tensor"),
        P("tensor", "dp"),
        P(),
        P(),
        P(),
        P("dp", "tensor"),
        P("tensor"),
        P("tensor", "dp"),
    )
    return jax.shard_map(
        body,
        mesh=mesh,
        in_specs=placed,
        out_specs=(
            P(("dp", "tensor"), None),
            P(("dp", "tensor"), None),
            P(),
            P(None, "dp", "tensor"),
            P(None, "dp", "tensor"),
            P(None, "tensor"),
            P("tensor", "dp"),
            P(),
            P(),
            P(),
            P("dp", "tensor"),
            P("tensor"),
            P("tensor", "dp"),
        ),
        check_vma=False,
    )
```

profile of v0, /device:TPU:0, one launch (start us, length us, event | category | flops | bytes accessed | tf_op | source)
XLA Modules:
  0.0 1115.1 jit_solution(101235424436037085)
XLA Ops:
  12.4 26.4 %all_gather.35 = bf16[384,768]{0,1:T(8,128)(2,1)} all-gather(bf16[384,48]{0,1:T(8,128)(2,1)} %param.27), channel_id=1, replica_groups=mesh['dp'=16,'tensor'=2] {'dp'}, dimensions={1}, use_global_device_ids=true | all-gather | bytes 626688 | tf_op jit(solution)/shard_map/all_gather | solution.py:31
  39.5 40.6 %all-gather.13.cloned.1.call-done = bf16[2,768,384]{2,1,0:T(8,128)(2,1)} async-done(((bf16[2,48,384]{2,1,0:T(8,128)(2,1)}), bf16[2,768,384]{2,1,0:T(8,128)(2,1)}) %all-gather.13.cloned.1.call-update) | async-done | bytes 1179664 | tf_op jit(solution)/shard_map/all_gather | solution.py:30
  84.6 39.5 %all-gather.9.cloned.1.call-done = bf16[4,768,384]{2,1,0:T(8,128)(2,1)} async-done(((bf16[4,48,384]{2,1,0:T(8,128)(2,1)}), bf16[4,768,384]{2,1,0:T(8,128)(2,1)}) %all-gather.9.cloned.1.call-update) | async-done | bytes 2359312 | tf_op jit(solution)/shard_map/all_gather | solution.py:29
  124.1 4.9 add_bitcast_fusion
  139.7 43.3 %while.30 = (s32[]{:T(128)}, bf16[2,512,384]{2,1,0:T(8,128)(2,1)}, f32[2,6,512]{2,1,0:T(8,128)S(1)}, s32[2,512]{1,0:T(2,128)S(1)}, s32[1024]{0:T(1024)S(1)}, /*i...) while((s32[]{:T(128)}, bf16[2,512,384]{2,1,0:T(8,128)(2,1)}, ...), condition=%wide.region_3.4_spmd.clone, body=%wide.region_0.3_spmd.clone.sunk | while | flops 1238561792 | bytes 69204112 | solution.py:136
  140.4 6.4 fusion.194
  146.8 6.6 fusion.196
  156.3 4.0 fusion.198
  162.0 6.4 fusion.194
  168.4 6.6 fusion.196
  177.9 4.0 fusion.198
  187.3 24.1 %reduce-scatter.8.cloned.1.call-done = bf16[512,768]{1,0:T(8,128)(2,1)} async-done(((bf16[1024,768]{1,0:T(8,128)(2,1)}), bf16[512,768]{1,0:T(8,128)(2,1)}) %reduce-scatter.8.cloned.1.call-update) | async-done | bytes 786448 | tf_op jit(solution)/shard_map/reduce_scatter | solution.py:140
  216.7 39.1 %all-gather.17.cloned.1.call-done = bf16[768,1536]{1,0:T(8,128)(2,1)} async-done(((bf16[48,1536]{1,0:T(8,128)(2,1)}), bf16[768,1536]{1,0:T(8,128)(2,1)}) %all-gather.17.cloned.1.call-update) | async-done | bytes 2359312 | tf_op jit(solution)/shard_map/all_gather | solution.py:32
  255.9 27.9 %all-gather.15.cloned.1.call-done = bf16[1024,768]{1,0:T(8,128)(2,1)} async-done(((bf16[512,768]{1,0:T(8,128)(2,1)}), bf16[1024,768]{1,0:T(8,128)(2,1)}) %all-gather.15.cloned.1.call-update) | async-done | bytes 1572880 | tf_op jit(solution)/shard_map/all_gather | solution.py:151
  283.8 20.0 %multiply_convert_fusion.1 = (bf16[1024,1536]{1,0:T(8,128)(2,1)}, f32[1024,1536]{1,0:T(8,128)}, f32[1024,1536]{1,0:T(8,128)}) fusion(f32[1536]{0:T(1024)S(1)} %convert_element_type.203, bf16[1024,768]{1,0:T(8,128)(2,1)} %all-gather.15.cloned.1.call-done, bf16[768,1536]{1,0:T(8,128)(2,1)} %all-gather.17.cloned.1.call-done), kind=kOutput, calls=%fused_computation.84 | convolution fusion | flops 2519728128 | bytes 19666944 | tf_op jit(solution)/shard_map/dot_general | solution.py:152
  303.7 24.7 %all-gather.19.cloned.1.call-done = bf16[1536,768]{0,1:T(8,128)(2,1)} async-done(((bf16[1536,48]{0,1:T(8,128)(2,1)}), bf16[1536,768]{0,1:T(8,128)(2,1)}) %all-gather.19.cloned.1.call-update) | async-done | bytes 2359312 | tf_op jit(solution)/shard_map/all_gather | solution.py:33
  328.4 6.4 convolution_convert_fusion.2
  335.6 24.3 %reduce-scatter.10.cloned.1.call-done = bf16[512,768]{1,0:T(8,128)(2,1)} async-done(((bf16[1024,768]{1,0:T(8,128)(2,1)}), bf16[512,768]{1,0:T(8,128)(2,1)}) %reduce-scatter.10.cloned.1.call-update) | async-done | bytes 786448 | tf_op jit(solution)/shard_map/reduce_scatter | solution.py:157
  369.1 26.9 %all-gather.21.cloned.1.call-done = bf16[1024,768]{1,0:T(8,128)(2,1)} async-done(((bf16[512,768]{1,0:T(8,128)(2,1)}), bf16[1024,768]{1,0:T(8,128)(2,1)}) %all-gather.21.cloned.1.call-update) | async-done | bytes 1572880 | tf_op jit(solution)/shard_map/all_gather | solution.py:184
  395.9 10.9 convert_reduce_fusion
  412.4 26.2 %reduce-scatter.12.cloned.1.call-done = bf16[512,768]{1,0:T(8,128)(2,1)} async-done(((bf16[1024,768]{1,0:T(8,128)(2,1)}), bf16[512,768]{1,0:T(8,128)(2,1)}) %reduce-scatter.12.cloned.1.call-update) | async-done | bytes 786448 | tf_op jit(solution)/shard_map/reduce_scatter | solution.py:193
  446.5 27.3 %all-gather.23.cloned.1.call-done = bf16[1024,768]{1,0:T(8,128)(2,1)} async-done(((bf16[512,768]{1,0:T(8,128)(2,1)}), bf16[1024,768]{1,0:T(8,128)(2,1)}) %all-gather.23.cloned.1.call-update) | async-done | bytes 1572880 | tf_op jit(solution)/shard_map/all_gather | solution.py:207
  484.9 204.9 %while.31 = (s32[]{:T(128)}, f32[1024,6,64]{0,2,1:T(8,128)}, f32[1024,6,64]{0,2,1:T(8,128)S(1)}, bf16[2,512,384]{1,2,0:T(8,128)(2,1)}, bf16[2,512,384]{1,2,0:T(8...) while((s32[]{:T(128)}, f32[1024,6,64]{0,2,1:T(8,128)}, ...), condition=%wide.region_17.18_spmd.clone, body=%wide.region_15.17_spmd.clone.sunk | while | flops 3305127936 | bytes 233310560 | solution.py:266
  485.8 7.6 fusion.217
  495.2 7.7 subtract_exponential_fusion.3
  502.9 18.7 %fusion.220 = bf16[6,512,64]{1,2,0:T(8,128)(2,1)S(1)} fusion(bf16[1024,6,64]{0,2,1:T(8,128)(2,1)S(1)} %get-tuple-element.732, pred[1024]{0:T(1024)(128)(4,1)S(1)} %get-tuple-element.726, f32[6,512,1024]{2,1,0:T(8,128)} %subtract_exponential_fusion.3, f32[6,512,1024]{2,1,0:T(8,128)} %fusion.217), kind=kOutput, calls=%fused_computation.45.clone.1 | convolution fusion | flops 418779136 | bytes 26346496 | tf_op jit(solution)/shard_map/while/body/eval_jaxpr/hqk,khd->qhd/dot_general | solution.py:241
  521.6 19.4 %fusion.219 = bf16[6,512,64]{1,2,0:T(8,128)(2,1)} fusion(bf16[1024,6,64]{0,2,1:T(8,128)(2,1)S(1)} %get-tuple-element.732, pred[1024]{0:T(1024)(128)(4,1)S(1)} %get-tuple-element.726, f32[6,512,1024]{2,1,0:T(8,128)} %subtract_exponential_fusion.3, f32[6,512,1024]{2,1,0:T(8,128)} %fusion.217), kind=kOutput, calls=%fused_computation.44.clone.1 | convolution fusion | flops 418779136 | bytes 26346496 | tf_op jit(solution)/shard_map/while/body/eval_jaxpr/hqk,khd->qhd/dot_general | solution.py:244
  542.9 6.1 bitcast_add_fusion.6
  549.0 19.3 %fusion.218 = f32[6,64,1024]{2,1,0:T(8,128)} fusion(pred[1024]{0:T(1024)(128)(4,1)S(1)} %get-tuple-element.726, f32[6,512,1024]{2,1,0:T(8,128)} %subtract_exponential_fusion.3, f32[6,512,1024]{2,1,0:T(8,128)} %fusion.217, bf16[2,512,6,64]{1,3,2,0:T(8,128)(2,1)} %get-tuple-element.725, s32[]{:T(128)S(6)} %copy.105), kind=kOutput, calls=%fused_computation.32.clone.1 | convolution fusion | flops 418385920 | bytes 52298756 | tf_op jit(solution)/shard_map/while/body/eval_jaxpr/hqk,qhd->khd/dot_general | solution.py:246
  568.4 18.7 %bitcast_add_fusion.5 = f32[1024,6,64]{0,2,1:T(8,128)} fusion(f32[1024,6,64]{0,2,1:T(8,128)} %get-tuple-element.703, f32[6,64,1024]{2,1,0:T(8,128)} %fusion.218, pred[1024]{0:T(1024)(128)(4,1)S(1)} %get-tuple-element.726, f32[6,512,1024]{2,1,0:T(8,128)} %subtract_exponential_fusion.3, f32[6,512,1024]{2,1,0:T(8,128)} %fusion.217, pred[]{:T(512)S(6)} %compare.3, ...), kind=kOutput, calls=%fused_computation.43.clone.1 | convolution fusion | flops 419958784 | bytes 55444484 | tf_op jit(solution)/shard_map/while/body/eval_jaxpr/hqk,qhd->khd/dot_general | solution.py:249
  587.9 7.6 fusion.217
  597.3 7.7 subtract_exponential_fusion.3
  605.0 18.7 %fusion.220 = bf16[6,512,64]{1,2,0:T(8,128)(2,1)S(1)} fusion(bf16[1024,6,64]{0,2,1:T(8,128)(2,1)S(1)} %get-tuple-element.732, pred[1024]{0:T(1024)(128)(4,1)S(1)} %get-tuple-element.726, f32[6,512,1024]{2,1,0:T(8,128)} %subtract_exponential_fusion.3, f32[6,512,1024]{2,1,0:T(8,128)} %fusion.217), kind=kOutput, calls=%fused_computation.45.clone.1 | convolution fusion | flops 418779136 | bytes 26346496 | tf_op jit(solution)/shard_map/while/body/eval_jaxpr/hqk,khd->qhd/dot_general | solution.py:241
  623.7 19.4 %fusion.219 = bf16[6,512,64]{1,2,0:T(8,128)(2,1)} fusion(bf16[1024,6,64]{0,2,1:T(8,128)(2,1)S(1)} %get-tuple-element.732, pred[1024]{0:T(1024)(128)(4,1)S(1)} %get-tuple-element.726, f32[6,512,1024]{2,1,0:T(8,128)} %subtract_exponential_fusion.3, f32[6,512,1024]{2,1,0:T(8,128)} %fusion.217), kind=kOutput, calls=%fused_computation.44.clone.1 | convolution fusion | flops 418779136 | bytes 26346496 | tf_op jit(solution)/shard_map/while/body/eval_jaxpr/hqk,khd->qhd/dot_general | solution.py:244
  645.0 6.1 bitcast_add_fusion.6
  651.1 19.3 %fusion.218 = f32[6,64,1024]{2,1,0:T(8,128)} fusion(pred[1024]{0:T(1024)(128)(4,1)S(1)} %get-tuple-element.726, f32[6,512,1024]{2,1,0:T(8,128)} %subtract_exponential_fusion.3, f32[6,512,1024]{2,1,0:T(8,128)} %fusion.217, bf16[2,512,6,64]{1,3,2,0:T(8,128)(2,1)} %get-tuple-element.725, s32[]{:T(128)S(6)} %copy.105), kind=kOutput, calls=%fused_computation.32.clone.1 | convolution fusion | flops 418385920 | bytes 52298756 | tf_op jit(solution)/shard_map/while/body/eval_jaxpr/hqk,qhd->khd/dot_general | solution.py:246
  670.4 19.1 %bitcast_add_fusion.5 = f32[1024,6,64]{0,2,1:T(8,128)} fusion(f32[1024,6,64]{0,2,1:T(8,128)} %get-tuple-element.703, f32[6,64,1024]{2,1,0:T(8,128)} %fusion.218, pred[1024]{0:T(1024)(128)(4,1)S(1)} %get-tuple-element.726, f32[6,512,1024]{2,1,0:T(8,128)} %subtract_exponential_fusion.3, f32[6,512,1024]{2,1,0:T(8,128)} %fusion.217, pred[]{:T(512)S(6)} %compare.3, ...), kind=kOutput, calls=%fused_computation.43.clone.1 | convolution fusion | flops 419958784 | bytes 55444484 | tf_op jit(solution)/shard_map/while/body/eval_jaxpr/hqk,qhd->khd/dot_general | solution.py:249
  706.3 6.8 convolution_bitcast_fusion
  713.1 6.6 copy.68
  719.7 4.4 convolution_bitcast_fusion.2
  724.1 5.3 copy.70
  733.4 6.3 fusion.128
  741.1 6.8 fusion.127
  755.0 42.7 %all-reduce.2 = (f32[5]{0:T(128)S(1)}, f32[5,768]{1,0:T(8,128)S(1)}, f32[2,768]{1,0:T(2,128)}, f32[2,768]{1,0:T(2,128)}, f32[2,768]{1,0:T(2,128)}, /*index=5*/f32[3072]{0:T(1024)S(1)}) all-reduce(f32[5]{0:T(128)S(1)} %stack.56, ...), channel_id=1, replica_groups=mesh['dp'=16,'tensor'=2] {'dp','tensor'}, use_global_device_ids=true, to_apply=%region_24.25 | all-reduce | flops 11525 | bytes 92200 | tf_op jit(solution)/shard_map/psum | solution.py:312
  803.3 84.8 %all-reduce.6.cloned.1.call-done = (f32[4,768,384]{2,0,1:T(4,128)}, f32[2,768,384]{2,0,1:T(2,128)}) async-done(((f32[4,768,384]{2,0,1:T(4,128)}, f32[2,768,384]{2,0,1:T(2,128)}), (f32[4,768,384]{2,0,1:T(4,128)}, f32[2,768,384]{2,0,1:T(2,128)})) %all-reduce.6.cloned.1.call-update) | async-done | bytes 7077904
  891.4 58.9 %reduce-scatter.16.cloned.1.call-done = f32[384,48]{0,1:T(8,128)} async-done(((f32[384,768]{0,1:T(8,128)}), f32[384,48]{0,1:T(8,128)}) %reduce-scatter.16.cloned.1.call-update) | async-done | bytes 73744 | tf_op jit(solution)/shard_map/reduce_scatter | solution.py:305
  950.3 79.0 %reduce-scatter.20.cloned.1.call-done = f32[1536,48]{0,1:T(8,128)} async-done(((f32[1536,768]{0,1:T(8,128)}), f32[1536,48]{0,1:T(8,128)}) %reduce-scatter.20.cloned.1.call-update) | async-done | bytes 294928 | tf_op jit(solution)/shard_map/reduce_scatter | solution.py:307
  1029.2 79.1 %reduce-scatter.18.cloned.1.call-done = f32[48,1536]{1,0:T(8,128)} async-done(((f32[768,1536]{1,0:T(8,128)}), f32[48,1536]{1,0:T(8,128)}) %reduce-scatter.18.cloned.1.call-update) | async-done | bytes 294928 | tf_op jit(solution)/shard_map/reduce_scatter | solution.py:306
  (239 shorter events, 119.0 us)
Async XLA Ops:
  7.2 32.3 %all-gather.11.cloned.1.call-start = ((), (), s32[]{:S(2)}) async-start(), calls=%async_computation.8 | async-start | bytes 2359296 | tf_op jit(solution)/shard_map/all_gather | solution.py:94
  7.9 72.2 %all-gather.13.cloned.1.call-start = ((), (), s32[]{:S(2)}) async-start(), calls=%async_computation.9 | async-start | bytes 1253376 | tf_op jit(solution)/shard_map/all_gather | solution.py:30
  8.7 115.4 %all-gather.9.cloned.1.call-start = ((), (), s32[]{:S(2)}) async-start(), calls=%async_computation.7 | async-start | bytes 2506752 | tf_op jit(solution)/shard_map/all_gather | solution.py:29
  9.4 202.0 %reduce-scatter.8.cloned.1.call-start = ((), (), s32[]{:S(2)}) async-start(), calls=%async_computation.10 | async-start | bytes 2359296 | tf_op jit(solution)/shard_map/reduce_scatter | solution.py:140
  83.4 40.7 %copy-start.38 = (bf16[1024,768]{1,0:T(8,128)(2,1)S(1)}, bf16[1024,768]{1,0:T(8,128)(2,1)}, u32[]{:S(2)}) copy-start(bf16[1024,768]{1,0:T(8,128)(2,1)} %all-gather.11.cloned.1.call-done) | copy-start | bytes 4718596
  136.5 3.2 copy-start.17
  139.7 43.4 %copy-start.16 = (bf16[384,768]{0,1:T(8,128)(2,1)S(1)}, bf16[384,768]{0,1:T(8,128)(2,1)}, u32[]{:S(2)}) copy-start(bf16[384,768]{0,1:T(8,128)(2,1)} %all_gather.35) | copy-start | bytes 1769476
  183.1 4.1 copy-start.30
  183.1 4.1 copy-start.31
  183.1 4.1 copy-start.32
  183.1 28.3 %copy-start = (bf16[512,768]{1,0:T(8,128)(2,1)S(1)}, bf16[512,768]{1,0:T(8,128)(2,1)}, u32[]{:S(2)}) copy-start(bf16[512,768]{1,0:T(8,128)(2,1)} %param.19) | copy-start | bytes 2359300
  186.5 69.3 %all-gather.17.cloned.1.call-start = ((), (), s32[]{:S(2)}) async-start(), calls=%async_computation.12 | async-start | bytes 2506752 | tf_op jit(solution)/shard_map/all_gather | solution.py:32
  187.1 96.7 %all-gather.15.cloned.1.call-start = ((), (), s32[]{:S(2)}) async-start(), calls=%async_computation.11 | async-start | bytes 2359296 | tf_op jit(solution)/shard_map/all_gather | solution.py:151
  211.4 3.1 copy-start.1
  211.4 5.3 copy-start.35
  215.9 112.5 %all-gather.19.cloned.1.call-start = ((), (), s32[]{:S(2)}) async-start(), calls=%async_computation.13 | async-start | bytes 2506752 | tf_op jit(solution)/shard_map/all_gather | solution.py:33
  216.6 143.2 %reduce-scatter.10.cloned.1.call-start = ((), (), s32[]{:S(2)}) async-start(), calls=%async_computation.14 | async-start | bytes 2359296 | tf_op jit(solution)/shard_map/reduce_scatter | solution.py:157
  328.4 6.5 copy-start.33
  334.8 61.1 %all-gather.21.cloned.1.call-start = ((), (), s32[]{:S(2)}) async-start(), calls=%async_computation.15 | async-start | bytes 2359296 | tf_op jit(solution)/shard_map/all_gather | solution.py:184
  359.9 2.3 copy-start.6
  359.9 2.3 copy-start.10
  368.6 70.1 %reduce-scatter.12.cloned.1.call-start = ((), (), s32[]{:S(2)}) async-start(), calls=%async_computation.16 | async-start | bytes 2359296 | tf_op jit(solution)/shard_map/reduce_scatter | solution.py:193
  395.9 12.7 %copy-start.37 = (bf16[768,1536]{1,0:T(8,128)(2,1)S(1)}, bf16[768,1536]{1,0:T(8,128)(2,1)}, u32[]{:S(2)}) copy-start(bf16[768,1536]{1,0:T(8,128)(2,1)} %all-gather.17.cloned.1.call-done) | copy-start | bytes 7077892
  412.4 61.4 %all-gather.23.cloned.1.call-start = ((), (), s32[]{:S(2)}) async-start(), calls=%async_computation.17 | async-start | bytes 2359296 | tf_op jit(solution)/shard_map/all_gather | solution.py:207
  438.7 3.8 copy-start.3
  438.7 3.8 copy-start.11
  443.5 33.6 %copy-start.22 = (f32[512]{0:T(512)}, f32[512]{0:T(512)S(1)}, u32[]{:S(2)}) copy-start(f32[512]{0:T(512)S(1)} %negate_multiply_fusion.1) | copy-start | bytes 6148
  446.4 354.3 %reduce-scatter.14.cloned.1.call-start = ((), (), s32[]{:S(2)}) async-start(), calls=%async_computation.18 | async-start | bytes 2359296 | tf_op jit(solution)/shard_map/reduce_scatter | solution.py:294
  485.0 8.3 copy-start.18
  485.0 8.3 copy-start.20
  568.4 18.8 %copy-start.19 = (f32[2,6,512]{2,1,0:T(8,128)S(1)}, f32[2,6,512]{2,1,0:T(8,128)}, u32[]{:S(2)}) copy-start(f32[2,6,512]{2,1,0:T(8,128)} %copy-done.18) | copy-start | bytes 73732 | tf_op jit(solution)/shard_map/while
  568.4 18.8 %copy-start.21 = (pred[1024]{0:T(1024)(128)(4,1)S(1)}, pred[1024]{0:T(1024)(128)(4,1)}, u32[]{:S(2)}) copy-start(pred[1024]{0:T(1024)(128)(4,1)} %copy-done.20) | copy-start | bytes 3076 | tf_op jit(solution)/shard_map/while
  587.1 8.3 copy-start.18
  587.1 8.3 copy-start.20
  670.4 19.2 %copy-start.19 = (f32[2,6,512]{2,1,0:T(8,128)S(1)}, f32[2,6,512]{2,1,0:T(8,128)}, u32[]{:S(2)}) copy-start(f32[2,6,512]{2,1,0:T(8,128)} %copy-done.18) | copy-start | bytes 73732 | tf_op jit(solution)/shard_map/while
  670.4 19.2 %copy-start.21 = (pred[1024]{0:T(1024)(128)(4,1)S(1)}, pred[1024]{0:T(1024)(128)(4,1)}, u32[]{:S(2)}) copy-start(pred[1024]{0:T(1024)(128)(4,1)} %copy-done.20) | copy-start | bytes 3076 | tf_op jit(solution)/shard_map/while
  699.1 4.5 copy-start.7
  699.1 4.5 copy-start.8
  700.9 2.7 copy-start.14
  700.9 2.7 copy-start.15
  701.0 2.7 copy-start.40
  706.2 181.8 %all-reduce.6.cloned.1.call-start = ((), (), s32[]{:S(2)}) async-start(), calls=%async_computation.22 | async-start | bytes 14155776
  729.4 3.9 copy-start.39
  729.4 220.8 %reduce-scatter.16.cloned.1.call-start = ((), (), s32[]{:S(2)}) async-start(), calls=%async_computation.19 | async-start | bytes 1253376 | tf_op jit(solution)/shard_map/reduce_scatter | solution.py:305
  733.3 295.9 %reduce-scatter.20.cloned.1.call-start = ((), (), s32[]{:S(2)}) async-start(), calls=%async_computation.21 | async-start | bytes 5013504 | tf_op jit(solution)/shard_map/reduce_scatter | solution.py:307
  739.7 368.6 %reduce-scatter.18.cloned.1.call-start = ((), (), s32[]{:S(2)}) async-start(), calls=%async_computation.20 | async-start | bytes 5013504 | tf_op jit(solution)/shard_map/reduce_scatter | solution.py:306
  747.9 52.8 %copy-start.5 = (f32[512,768]{1,0:T(8,128)S(1)}, f32[512,768]{1,0:T(8,128)}, u32[]{:S(2)}) copy-start(f32[512,768]{1,0:T(8,128)} %copy-done.4) | copy-start | bytes 4718596
  747.9 52.8 %copy-start.23 = (f32[512]{0:T(512)S(1)}, f32[512]{0:T(512)}, u32[]{:S(2)}) copy-start(f32[512]{0:T(512)} %copy-done.22) | copy-start | bytes 6148
  (14 other events, 20.4 us)
Sparse Core Ops, SparseCore 0:
  9.5 29.9 all-gather.10
  41.7 38.3 all-gather.12
  82.3 41.7 all-gather.8
  186.6 24.7 reduce-scatter.7
  213.5 42.2 all-gather.16
  257.8 25.8 all-gather.14
  286.0 42.3 all-gather.18
  334.9 24.8 reduce-scatter.9
  368.7 27.1 all-gather.20
  412.5 26.1 reduce-scatter.11
  446.5 27.1 all-gather.22
  706.4 26.1 reduce-scatter.13
  736.3 151.7 all-reduce.5
  892.1 58.1 reduce-scatter.15
  954.5 74.6 reduce-scatter.19
  1033.5 74.7 reduce-scatter.17
where the time goes:
time: 1120 us
  waiting for transfers between devices  607 us (54%)
  matrix products  322 us (29%)
  blocking collectives  69.1 us (6%)
  local copies, waits for them, and re-layouts  58.4 us (5%)
  other arithmetic  41 us (4%)
  between operations  16.1 us (1%)
    unnamed x17, waiting for transfers between devices  88.3 us
    reduce_scatter x1, waiting for transfers between devices, body(): lax.psum_scatter(up_grad, 'dp', scatter_dimension=0, tiled=True)  79.1 us
    reduce_scatter x1, waiting for transfers between devices, body(): lax.psum_scatter(down_grad, 'dp', scatter_dimension=1, tiled=True)  79 us
    reduce_scatter x1, waiting for transfers between devices, body(): lax.psum_scatter(out_grad, 'dp', scatter_dimension=1, tiled=True)  58.9 us
    psum x1, blocking collectives, body(): lax.psum((jnp.stack([gain_one, gain_two]), jnp.stack([shift_one, shift_tw...  42.7 us
    all_gather x1, waiting for transfers between devices, fetch_weights(): lax.all_gather(key_value_weight, 'dp', axis=1, tiled=True)  40.6 us
    all_gather x1, waiting for transfers between devices, fetch_weights(): lax.all_gather(query_weight, 'dp', axis=1, tiled=True)  39.5 us
    all_gather x1, waiting for transfers between devices, fetch_weights(): lax.all_gather(up_weight, 'dp', axis=0, tiled=True)  39.1 us
  transfers between devices with their start and end apart: 16, of which 15 were waited for; matrix products, arithmetic and copies ran while one was open for 8% of the time, Pallas kernels for 0%

commit v1 on v0

v1 whole, which is shorter than its diff:
```python
import functools

import jax
import jax.numpy as jnp
from jax import lax
from jax.experimental import pallas as pl
from jax.experimental.pallas import tpu as pltpu
from jax.sharding import PartitionSpec as P

HEAD = 64
EPS = 1e-06
NEG = -1e30
GRID = 16
LANES = 128
MESH = pl.DeviceIdType.MESH
BF16 = jnp.bfloat16
F32 = jnp.float32
VMEM_LIMIT = 60 * 1024 * 1024


def layer_norm(resid, gain, shift):
    center = resid - jnp.mean(resid, -1, keepdims=True)
    spread = jnp.mean(center * center, -1, keepdims=True)
    return center * lax.rsqrt(spread + EPS) * gain + shift


def gelu_exact(values):
    return jax.nn.gelu(values, approximate=False)


class Place:
    def __init__(self, subs):
        rank = lax.axis_index("dp")
        self.subs = subs
        self.sub = rank % subs
        block = rank // subs
        self.z = block // 4
        self.x = (block // 2) % 2
        self.c = block % 2
        self.y = lax.axis_index("tensor")
        self.x1 = jnp.where(self.c == 0, 1 - self.x, self.x)
        self.y1 = jnp.where(self.c == 0, self.y, 1 - self.y)
        self.x2 = jnp.where(self.c == 0, self.x, 1 - self.x)
        self.y2 = jnp.where(self.c == 0, 1 - self.y, self.y)

    def device(self, z=None, x=None, c=None, y=None):
        z = self.z if z is None else z
        x = self.x if x is None else x
        c = self.c if c is None else c
        y = self.y if y is None else y
        return (((z * 2 + x) * 2 + c) * self.subs + self.sub, y)

    def z_peer(self, step):
        return self.device(z=(self.z + step) % 4)

    def first(self):
        return self.device(x=self.x1, y=self.y1)

    def second(self):
        return self.device(x=self.x2, y=self.y2)

    def sibling(self):
        return self.device(c=1 - self.c)

    def pieces(self):
        return (
            (self.x, self.y),
            (self.x1, self.y1),
            (self.x2, self.y2),
            (1 - self.x, 1 - self.y),
        )


def entry_barrier(place):
    barrier = pltpu.get_barrier_semaphore()
    peers = [place.z_peer(step) for step in (1, 2, 3)]
    peers += [place.device(x=1 - place.x), place.device(y=1 - place.y), place.sibling()]
    for peer in peers:
        pl.semaphore_signal(barrier, inc=1, device_id=peer, device_id_type=MESH)
    pl.semaphore_wait(barrier, len(peers))


def remote(src, dst, send, recv, peer):
    return pltpu.make_async_remote_copy(
        src_ref=src, dst_ref=dst, send_sem=send, recv_sem=recv, device_id=peer, device_id_type=MESH
    )


class Gather:
    def __init__(self, place, shard, full, send, recv, local):
        self.place, self.shard, self.full = place, shard, full
        self.send, self.recv, self.local = send, recv, local
        self.w = shard.shape[-1]
        self.started = []

    def cols(self, y):
        return pl.ds(pl.multiple_of(y * self.w, LANES), self.w)

    def piece(self, spot, c):
        x, y = spot
        return self.full.at[:, :, x, c, :, self.cols(y)]

    def copy(self, index, src, dst, peer):
        step = remote(src, dst, self.send.at[index], self.recv.at[index], peer)
        step.start()
        self.started.append(step)

    def arrive(self, index, ref):
        remote(ref, ref, self.send.at[index], self.recv.at[index], self.place.sibling()).wait_recv()

    def own(self, z):
        p = self.place
        return self.full.at[:, z, p.x, p.c, :, self.cols(p.y)]

    def stage1(self):
        p = self.place
        self.kept = pltpu.make_async_copy(self.shard, self.own(p.z), self.local)
        self.kept.start()
        for step in (1, 2, 3):
            self.copy(step - 1, self.shard, self.own(p.z), p.z_peer(step))

    def stage2(self):
        p = self.place
        self.kept.wait()
        for step in (1, 2, 3):
            self.arrive(step - 1, self.own((p.z + 4 - step) % 4))
        mine = self.piece(p.pieces()[0], p.c)
        self.copy(3, mine, mine, p.first())
        self.copy(4, mine, mine, p.second())
        self.copy(6, mine, mine, p.sibling())

    def stage3(self):
        p = self.place
        got = self.piece(p.pieces()[1], p.c)
        self.arrive(3, got)
        self.copy(5, got, got, p.second())
        self.copy(7, got, got, p.sibling())

    def stage4(self):
        p = self.place
        for index, spot in ((4, 2), (5, 3)):
            got = self.piece(p.pieces()[spot], p.c)
            self.arrive(index, got)
            self.copy(index + 4, got, got, p.sibling())

    def stage5(self):
        p = self.place
        spots = p.pieces()
        for index, spot in ((6, 0), (7, 2), (8, 1), (9, 3)):
            self.arrive(index, self.piece(spots[spot], 1 - p.c))
        for step in self.started:
            step.wait_send()

    def stages(self):
        return [self.stage1, self.stage2, self.stage3, self.stage4, self.stage5]


def wavefront(movers):
    lists = [mover.stages() for mover in movers]
    depth = max(len(stages) for stages in lists)
    order = []
    for time in range(len(lists) + depth - 1):
        for index in range(len(lists)):
            stage = time - index
            if 0 <= stage < len(lists[index]):
                order.append(lists[index][stage])
    return order


def gather_kernel(subs, count, *refs):
    shards, rows = refs[:count], refs[count]
    fulls, both = refs[count + 1 : 2 * count + 1], refs[2 * count + 1]
    send, recv, local, row_sems = refs[2 * count + 2 :]
    place = Place(subs)
    entry_barrier(place)
    kept = pltpu.make_async_copy(rows, both.at[place.y], row_sems.at[0])
    kept.start()
    across = remote(
        rows, both.at[place.y], row_sems.at[1], row_sems.at[2], place.device(y=1 - place.y)
    )
    across.start()
    movers = [
        Gather(place, shards[i], fulls[i], send.at[i], recv.at[i], local.at[i]) for i in range(count)
    ]
    for mover in movers:
        mover.stage1()
    for step in wavefront(movers):
        if step.__func__ is not Gather.stage1:
            step()
    kept.wait()
    across.wait()


def gather_weights(subs, shards, rows):
    count = len(shards)
    outs = [
        jax.ShapeDtypeStruct((s.shape[0], 4, 2, 2, s.shape[1], 2 * s.shape[2]), BF16) for s in shards
    ]
    outs.append(jax.ShapeDtypeStruct((2,) + rows.shape, BF16))
    results = pl.pallas_call(
        functools.partial(gather_kernel, subs, count),
        out_shape=outs,
        in_specs=[pl.BlockSpec(memory_space=pltpu.VMEM)] * (count + 1),
        out_specs=[pl.BlockSpec(memory_space=pl.ANY)] * (count + 1),
        scratch_shapes=[
            pltpu.SemaphoreType.DMA((count, 10)),
            pltpu.SemaphoreType.DMA((count, 10)),
            pltpu.SemaphoreType.DMA((count,)),
            pltpu.SemaphoreType.DMA((3,)),
        ],
        compiler_params=pltpu.CompilerParams(
            collective_id=0, has_side_effects=True, vmem_limit_bytes=VMEM_LIMIT
        ),
        name="gather_weights",
    )(*shards, rows)
    fulls = [r.reshape(r.shape[0], GRID * r.shape[4], r.shape[5]) for r in results[:count]]
    return fulls, results[count]


class Scatter:
    def __init__(self, place, part, total, mine, from_core, from_second, from_first, from_z, send, recv, local):
        self.place, self.part, self.total = place, part, total
        self.mine, self.from_core = mine, from_core
        self.from_second, self.from_first, self.from_z = from_second, from_first, from_z
        self.send, self.recv, self.local = send, recv, local
        self.m, self.rows, self.w = total.shape
        self.started = []

    def cols(self, y):
        return pl.ds(pl.multiple_of(y * self.w, LANES), self.w)

    def copy(self, index, src, dst, peer):
        step = remote(src, dst, self.send.at[index], self.recv.at[index], peer)
        step.start()
        self.started.append(step)

    def arrive(self, index, ref):
        remote(ref, ref, self.send.at[index], self.recv.at[index], self.place.sibling()).wait_recv()

    def add(self, target, source):
        m = self.m

        def step(index, carry):
            i, z = index // 4, index % 4
            target[i, z] = (target[i, z].astype(F32) + source[i, z].astype(F32)).astype(BF16)
            return carry

        lax.fori_loop(0, m * 4, step, 0)

    def stage1(self):
        p = self.place
        spots = p.pieces()
        self.kept = []
        for slot, (here, there) in enumerate(((3, 3), (2, 1), (1, 2), (0, 0))):
            x, y = spots[here]
            keep = pltpu.make_async_copy(
                self.part.at[:, :, x, p.c, :, self.cols(y)], self.mine.at[slot], self.local.at[slot]
            )
            keep.start()
            self.kept.append(keep)
            x, y = spots[there]
            self.copy(
                slot,
                self.part.at[:, :, x, 1 - p.c, :, self.cols(y)],
                self.from_core.at[slot],
                p.sibling(),
            )

    def joined(self, slot):
        self.kept[slot].wait()
        self.arrive(slot, self.from_core.at[slot])
        self.add(self.mine.at[slot], self.from_core.at[slot])

    def stage2(self):
        p = self.place
        for slot in (0, 1):
            self.joined(slot)
            self.copy(4 + slot, self.mine.at[slot], self.from_second.at[slot], p.second())
        for slot in (2, 3):
            self.joined(slot)

    def stage3(self):
        p = self.place
        self.arrive(4, self.from_second.at[0])
        self.add(self.mine.at[2], self.from_second.at[0])
        self.copy(6, self.mine.at[2], self.from_first, p.first())
        self.arrive(5, self.from_second.at[1])
        self.add(self.mine.at[3], self.from_second.at[1])

    def stage4(self):
        p = self.place
        self.arrive(6, self.from_first)
        self.add(self.mine.at[3], self.from_first)
        for step in (1, 2, 3):
            self.copy(
                6 + step, self.mine.at[3, :, (p.z + step) % 4], self.from_z.at[step - 1], p.z_peer(step)
            )

    def stage5(self):
        p = self.place
        for step in (1, 2, 3):
            self.arrive(6 + step, self.from_z.at[step - 1])

        def step(i, carry):
            total = self.mine[3, i, p.z].astype(F32)
            for s in range(3):
                total = total + self.from_z[s, i].astype(F32)
            self.total[i] = total
            return carry

        lax.fori_loop(0, self.m, step, 0)
        for step in self.started:
            step.wait_send()

    def stages(self):
        return [self.stage1, self.stage2, self.stage3, self.stage4, self.stage5]


class Sum:
    def __init__(self, place, source, total, box, send, recv):
        self.place, self.source, self.total = place, source, total
        self.box, self.send, self.recv = box, send, recv

    def hop(self, index):
        p = self.place
        flip = p.z + 1 - 2 * (p.z % 2)
        far = (p.z + 2) % 4
        peers = (p.sibling(), p.device(x=1 - p.x), p.device(y=1 - p.y), p.device(z=flip), p.device(z=far))
        if index < 5:
            src = self.source if index == 0 else self.total.at[index - 1]
            step = remote(src, self.box.at[index], self.send.at[index], self.recv.at[index], peers[index])
            step.start()
            self.flying = step

    def land(self, index):
        self.flying.wait()
        src = self.source if index == 0 else self.total.at[index - 1]
        self.total[index] = src[...] + self.box[index]

    def stages(self):
        def first():
            self.hop(0)

        def later(index):
            self.land(index)
            self.hop(index + 1)

        return [first] + [functools.partial(later, i) for i in range(5)]


def scatter_scratch(shape):
    m, rows, w = shape
    return [
        pltpu.VMEM((4, m, 4, rows, w), BF16),
        pltpu.VMEM((4, m, 4, rows, w), BF16),
        pltpu.VMEM((2, m, 4, rows, w), BF16),
        pltpu.VMEM((m, 4, rows, w), BF16),
        pltpu.VMEM((3, m, rows, w), BF16),
        pltpu.SemaphoreType.DMA((10,)),
        pltpu.SemaphoreType.DMA((10,)),
        pltpu.SemaphoreType.DMA((4,)),
    ]


def scatter_kernel(subs, count, *refs):
    parts, small = refs[:count], refs[count]
    totals, small_total = refs[count + 1 : 2 * count + 1], refs[2 * count + 1]
    scratch = refs[2 * count + 2 :]
    place = Place(subs)
    entry_barrier(place)
    movers = [
        Scatter(place, parts[i], totals[i], *scratch[8 * i : 8 * i + 8]) for i in range(count)
    ]
    running, box, send, recv = scratch[8 * count :]
    small_sum = Sum(place, small, running, box, send, recv)
    for mover in movers:
        mover.stage1()
    steps = [s for s in wavefront(movers) if s.__func__ is not Scatter.stage1]
    extra = small_sum.stages()
    for index, step in enumerate(steps):
        if index < len(extra):
            extra[index]()
        step()
    for step in extra[len(steps) :]:
        step()
    small_total[...] = running[4]


def scatter_gradients(subs, parts, small):
    count = len(parts)
    rows = parts[0].shape[1] // GRID
    shaped = [p.reshape(p.shape[0], 4, 2, 2, rows, p.shape[2]) for p in parts]
    shapes = [(p.shape[0], rows, p.shape[2] // 2) for p in parts]
    outs = [jax.ShapeDtypeStruct(s, F32) for s in shapes]
    outs.append(jax.ShapeDtypeStruct(small.shape, F32))
    scratch = []
    for s in shapes:
        scratch += scatter_scratch(s)
    scratch += [
        pltpu.VMEM((5,) + small.shape, F32),
        pltpu.VMEM((5,) + small.shape, F32),
        pltpu.SemaphoreType.DMA((5,)),
        pltpu.SemaphoreType.DMA((5,)),
    ]
    results = pl.pallas_call(
        functools.partial(scatter_kernel, subs, count),
        out_shape=outs,
        in_specs=[pl.BlockSpec(memory_space=pl.ANY)] * count + [pl.BlockSpec(memory_space=pltpu.VMEM)],
        out_specs=[pl.BlockSpec(memory_space=pltpu.VMEM)] * (count + 1),
        scratch_shapes=scratch,
        compiler_params=pltpu.CompilerParams(
            collective_id=1, has_side_effects=True, vmem_limit_bytes=VMEM_LIMIT
        ),
        name="scatter_gradients",
    )(*shaped, small)
    return results[:count], results[count]


def head_lanes(half):
    lane = lax.broadcasted_iota(jnp.int32, (1, LANES), 1)
    return (lane // HEAD) == half


def dot_nt(a, b):
    return lax.dot_general(a, b, (((1,), (1,)), ((), ())), preferred_element_type=F32)


def dot_nn(a, b):
    return lax.dot_general(a, b, (((1,), (0,)), ((), ())), preferred_element_type=F32)


def forward_kernel(qw, qe, keys, values, seg_col, valid_col, ent_col, seg_row, pos_row, ctx, probs, bias):
    length, rows = bias.shape

    @pl.when(pl.program_id(0) == 0)
    def _():
        spot = lax.broadcasted_iota(jnp.int32, (length, rows), 0)
        same = seg_col[...] == seg_row[...]
        seen = (valid_col[...] == 1) | (spot == pos_row[...])
        bias[...] = jnp.where(same & seen, 0.0, NEG)

    queries = jnp.concatenate([qw[...], qe[...]], axis=1)
    key = keys[...]
    ent = ent_col[...] == 1
    zero = jnp.zeros_like(key)
    turned = values[...].T
    for half in range(2):
        lanes = head_lanes(half)
        wide = jnp.concatenate(
            [jnp.where(lanes & ~ent, key, zero), jnp.where(lanes & ent, key, zero)], axis=1
        )
        scores = dot_nt(wide, queries) + bias[...]
        top = jnp.max(scores, axis=0, keepdims=True)
        expo = jnp.exp(scores - top)
        total = jnp.sum(expo, axis=0, keepdims=True)
        prob = (expo * (1.0 / total)).astype(BF16)
        probs[half] = prob
        ctx[half * HEAD : (half + 1) * HEAD, :] = dot_nn(
            turned[half * HEAD : (half + 1) * HEAD, :], prob
        ).astype(BF16)


def attention_forward(qw, qe, keys, values, seg_col, valid_col, ent_col, seg_row, pos_row):
    rows, width = qw.shape
    length = keys.shape[0]
    pairs = width // LANES
    block = lambda n: pl.BlockSpec((n, LANES), lambda i: (0, i))
    whole = lambda a: pl.BlockSpec(a.shape, lambda i: (0,) * a.ndim)
    return pl.pallas_call(
        forward_kernel,
        grid=(pairs,),
        out_shape=[
            jax.ShapeDtypeStruct((width, rows), BF16),
            jax.ShapeDtypeStruct((2 * pairs, length, rows), BF16),
        ],
        in_specs=[block(rows), block(rows), block(length), block(length)]
        + [whole(a) for a in (seg_col, valid_col, ent_col, seg_row, pos_row)],
        out_specs=[
            pl.BlockSpec((LANES, rows), lambda i: (i, 0)),
            pl.BlockSpec((2, length, rows), lambda i: (i, 0, 0)),
        ],
        scratch_shapes=[pltpu.VMEM((length, rows), F32)],
        compiler_params=pltpu.CompilerParams(vmem_limit_bytes=VMEM_LIMIT),
        name="attention_forward",
    )(qw, qe, keys, values, seg_col, valid_col, ent_col, seg_row, pos_row)


def backward_kernel(probs, qw, qe, keys, values, ctx, dctx, ent_col, ent_row, dqw, dqe, dkeys, dvalues):
    queries = jnp.concatenate([qw[...], qe[...]], axis=1)
    value = values[...]
    turned = keys[...].T
    ent = ent_col[...] == 1
    ent_lane = ent_row[...] == 1
    grad = dctx[...]
    zero = jnp.zeros_like(value)
    dk, dv = [], []
    for half in range(2):
        lanes = head_lanes(half)
        here = slice(half * HEAD, (half + 1) * HEAD)
        prob = probs[half]
        delta = jnp.sum(
            ctx[here, :].astype(F32) * grad[here, :].astype(F32), axis=0, keepdims=True
        )
        dprob = dot_nn(jnp.where(lanes, value, zero), grad)
        dscore = (prob.astype(F32) * (dprob - delta)).astype(BF16)
        key_t = turned[here, :]
        none = jnp.zeros_like(key_t)
        tall = jnp.concatenate(
            [jnp.where(ent_lane, none, key_t), jnp.where(ent_lane, key_t, none)], axis=0
        )
        dq = dot_nn(tall, dscore) * (HEAD ** (-0.5))
        dqw[here, :] = dq[:HEAD].astype(BF16)
        dqe[here, :] = dq[HEAD:].astype(BF16)
        both = dot_nn(dscore, queries)
        dk.append(jnp.where(ent, both[:, LANES:], both[:, :LANES]))
        dv.append(dot_nt(prob, grad))
    dkeys[...] = jnp.where(head_lanes(0), dk[0], dk[1]).astype(BF16)
    dvalues[...] = jnp.where(head_lanes(0), dv[0], dv[1]).astype(BF16)


def attention_backward(probs, qw, qe, keys, values, ctx, dctx, ent_col, ent_row):
    rows, width = qw.shape
    length = keys.shape[0]
    pairs = width // LANES
    block = lambda n: pl.BlockSpec((n, LANES), lambda i: (0, i))
    turned = pl.BlockSpec((LANES, rows), lambda i: (i, 0))
    whole = lambda a: pl.BlockSpec(a.shape, lambda i: (0,) * a.ndim)
    return pl.pallas_call(
        backward_kernel,
        grid=(pairs,),
        out_shape=[
            jax.ShapeDtypeStruct((width, rows), BF16),
            jax.ShapeDtypeStruct((width, rows), BF16),
            jax.ShapeDtypeStruct((length, width), BF16),
            jax.ShapeDtypeStruct((length, width), BF16),
        ],
        in_specs=[
            pl.BlockSpec((2, length, rows), lambda i: (i, 0, 0)),
            block(rows),
            block(rows),
            block(length),
            block(length),
            turned,
            turned,
            whole(ent_col),
            whole(ent_row),
        ],
        out_specs=[turned, turned, block(length), block(length)],
        compiler_params=pltpu.CompilerParams(vmem_limit_bytes=VMEM_LIMIT),
        name="attention_backward",
    )(probs, qw, qe, keys, values, ctx, dctx, ent_col, ent_row)


def body(
    layer_input,
    grad_out,
    segment,
    entity,
    valid_mask,
    query_weight,
    key_value_weight,
    attn_bias,
    out_weight,
    out_bias,
    ln_gain,
    ln_bias,
    up_weight,
    ffn_bias,
    down_weight,
):
    rows, width = layer_input.shape
    length = segment.shape[0]
    rank = lax.axis_index("tensor")
    subs = lax.axis_size("dp") // GRID
    start = rank * rows

    shards = [
        query_weight,
        key_value_weight,
        out_weight.T[None],
        up_weight[None],
        down_weight.T[None],
    ]
    groups = [[b * subs + s for s in range(subs)] for b in range(GRID)]
    if subs > 1:
        shards = [
            lax.all_gather(s, "dp", axis=1, tiled=True, axis_index_groups=groups) for s in shards
        ]
    shards = [shards[1], shards[0]] + shards[2:]
    (w_kv, w_q, w_out_t, w_up, w_down_t), both = gather_weights(subs, shards, layer_input)
    w_out_t, w_up, w_down_t = w_out_t[0], w_up[0], w_down_t[0]
    bias_full = lax.all_gather(attn_bias, "tensor", axis=1, tiled=True).astype(F32)
    ffn_bias_full = lax.all_gather(ffn_bias, "tensor", axis=0, tiled=True).astype(F32)
    tokens = both.reshape(length, width)

    ent_own = lax.dynamic_slice_in_dim(entity, start, rows)
    valid_own = lax.dynamic_slice_in_dim(valid_mask, start, rows).astype(F32)[:, None]
    ent_flag = (ent_own == 1)[:, None]
    scale = HEAD ** (-0.5)
    four = jnp.einsum("ld,mde->mle", layer_input, w_q, preferred_element_type=F32)
    four = four + bias_full[:4, None, :]
    query_word = jnp.where(ent_flag, four[2], four[0]).astype(BF16) * BF16(scale)
    query_ent = jnp.where(ent_flag, four[3], four[1]).astype(BF16) * BF16(scale)
    keys = jnp.dot(tokens, w_kv[0], preferred_element_type=F32).astype(BF16)
    values = (jnp.dot(tokens, w_kv[1], preferred_element_type=F32) + bias_full[4]).astype(BF16)

    ent_col = entity[:, None]
    ent_row = entity[None, :]
    seg_row = lax.dynamic_slice_in_dim(segment, start, rows)[None, :]
    pos_row = (start + jnp.arange(rows, dtype=jnp.int32))[None, :]
    context_t, probs = attention_forward(
        query_word, query_ent, keys, values, segment[:, None], valid_mask[:, None], ent_col, seg_row, pos_row
    )

    attn = jnp.einsum("cl,dc->ld", context_t, w_out_t, preferred_element_type=F32)
    attn = attn + out_bias[0].astype(F32)
    resid_one = layer_input.astype(F32) + attn
    hidden, ln_one_pull = jax.vjp(
        layer_norm, resid_one, ln_gain[0].astype(F32), ln_bias[0].astype(F32)
    )
    hidden_low = hidden.astype(BF16)
    pre = jnp.dot(hidden_low, w_up, preferred_element_type=F32) + ffn_bias_full
    active, gelu_pull = jax.vjp(gelu_exact, pre)
    active_low = active.astype(BF16)
    ffn = jnp.einsum("lf,df->ld", active_low, w_down_t, preferred_element_type=F32)
    ffn = ffn + out_bias[1].astype(F32)
    resid_two = hidden + ffn
    result, ln_two_pull = jax.vjp(
        layer_norm, resid_two, ln_gain[1].astype(F32), ln_bias[1].astype(F32)
    )
    output = result.astype(BF16)
    stats = jnp.stack(
        [
            jnp.sum(valid_own * resid_one * resid_one),
            jnp.sum(valid_own * attn * attn),
            jnp.sum(valid_own * ffn * ffn),
            jnp.sum(valid_own * resid_two * resid_two),
            jnp.sum(valid_own),
        ]
    )

    d_two, gain_two, shift_two = ln_two_pull(grad_out.astype(F32))
    d_ffn = d_two.astype(BF16)
    bias_two = jnp.sum(d_ffn.astype(F32), 0)
    d_active = jnp.dot(d_ffn, w_down_t, preferred_element_type=F32)
    (d_pre,) = gelu_pull(d_active)
    d_pre_low = d_pre.astype(BF16)
    down_part = jnp.einsum("ld,lf->df", d_ffn, active_low, preferred_element_type=F32).astype(BF16)
    up_part = jnp.einsum("ld,lf->df", hidden_low, d_pre_low, preferred_element_type=F32).astype(BF16)
    ffn_bias_part = jnp.sum(d_pre_low.astype(F32), 0)
    d_hidden = d_two + jnp.einsum("lf,df->ld", d_pre_low, w_up, preferred_element_type=F32)
    d_one, gain_one, shift_one = ln_one_pull(d_hidden)
    d_attn = d_one.astype(BF16)
    bias_one = jnp.sum(d_attn.astype(F32), 0)
    d_context_t = jnp.einsum("ld,dc->cl", d_attn, w_out_t, preferred_element_type=F32).astype(BF16)
    out_part = jnp.einsum("ld,cl->dc", d_attn, context_t, preferred_element_type=F32).astype(BF16)

    d_word_t, d_ent_t, d_keys_all, d_values_all = attention_backward(
        probs, query_word, query_ent, keys, values, context_t, d_context_t, ent_col, ent_row
    )
    pairs = lax.axis_size("tensor")
    stacked = jnp.stack([d_keys_all, d_values_all]).reshape(2, 2, rows, width)
    mine = lax.dynamic_index_in_dim(stacked, rank, 1, keepdims=False)
    theirs = lax.dynamic_index_in_dim(stacked, 1 - rank, 1, keepdims=False)
    swapped = lax.ppermute(theirs, "tensor", [(i, pairs - 1 - i) for i in range(pairs)])
    d_kv = (mine.astype(F32) + swapped.astype(F32)).astype(BF16)

    ent_lane = (ent_own == 1)[None, :]
    none = jnp.zeros_like(d_word_t)
    d_queries_t = jnp.stack(
        [
            jnp.where(ent_lane, none, d_word_t),
            jnp.where(ent_lane, none, d_ent_t),
            jnp.where(ent_lane, d_word_t, none),
            jnp.where(ent_lane, d_ent_t, none),
        ]
    )
    query_part = jnp.einsum(
        "ld,mel->mde", layer_input, d_queries_t, preferred_element_type=F32
    ).astype(BF16)
    kv_part = jnp.einsum("ld,mle->mde", layer_input, d_kv, preferred_element_type=F32).astype(BF16)
    attn_bias_part = jnp.concatenate(
        [jnp.sum(d_queries_t.astype(F32), 2), jnp.sum(d_kv[1].astype(F32), 0)[None]], 0
    )
    input_grad = (
        d_one
        + jnp.einsum("mel,mde->ld", d_queries_t, w_q, preferred_element_type=F32)
        + jnp.einsum("mle,mde->ld", d_kv, w_kv, preferred_element_type=F32)
    )

    pieces = [
        gain_one,
        gain_two,
        shift_one,
        shift_two,
        bias_one,
        bias_two,
        attn_bias_part.reshape(-1),
        ffn_bias_part,
        stats,
    ]
    flat = jnp.concatenate(pieces)
    padded = -(-flat.shape[0] // (8 * LANES)) * 8 * LANES
    small = jnp.pad(flat, (0, padded - flat.shape[0])).reshape(-1, LANES)
    sums, small_sum = scatter_gradients(
        subs, [down_part[None], up_part[None], out_part[None], query_part, kv_part], small
    )
    if subs > 1:
        sums = [
            lax.psum_scatter(s, "dp", scatter_dimension=1, tiled=True, axis_index_groups=groups)
            for s in sums
        ]
        small_sum = lax.psum(small_sum, "dp", axis_index_groups=groups)
    down_sum, up_sum, out_sum, query_sum, kv_sum = sums
    flat = small_sum.reshape(-1)
    gains = flat[: 2 * width].reshape(2, width)
    shifts = flat[2 * width : 4 * width].reshape(2, width)
    out_biases = flat[4 * width : 6 * width].reshape(2, width)
    attn_biases = flat[6 * width : 11 * width].reshape(5, width)
    units = ffn_bias_full.shape[0]
    ffn_biases = flat[11 * width : 11 * width + units]
    stat_sum = flat[11 * width + units : 11 * width + units + 5]
    cols = attn_bias.shape[1]
    half = ffn_bias.shape[0]
    return (
        output,
        input_grad,
        jnp.sqrt(stat_sum[:4] / (stat_sum[4] * width)),
        query_sum,
        kv_sum,
        lax.dynamic_slice_in_dim(attn_biases, rank * cols, cols, 1),
        out_sum[0].T,
        out_biases,
        gains,
        shifts,
        up_sum[0],
        lax.dynamic_slice_in_dim(ffn_biases, rank * half, half, 0),
        down_sum[0].T,
    )


def solution(mesh):
    placed = (
        P(("dp", "tensor"), None),
        P(("dp", "tensor"), None),
        P("dp"),
        P("dp"),
        P("dp"),
        P(None, "dp", "tensor"),
        P(None, "dp", "tensor"),
        P(None, "tensor"),
        P("tensor", "dp"),
        P(),
        P(),
        P(),
        P("dp", "tensor"),
        P("tensor"),
        P("tensor", "dp"),
    )
    return jax.shard_map(
        body,
        mesh=mesh,
        in_specs=placed,
        out_specs=(
            P(("dp", "tensor"), None),
            P(("dp", "tensor"), None),
            P(),
            P(None, "dp", "tensor"),
            P(None, "dp", "tensor"),
            P(None, "tensor"),
            P("tensor", "dp"),
            P(),
            P(),
            P(),
            P("dp", "tensor"),
            P("tensor"),
            P("tensor", "dp"),
        ),
        check_vma=False,
    )
```

time: 1120 us -> 393 us (0.35)
  waiting for transfers between devices: 607 us -> 5.88 us
  Pallas kernels: 0 us -> 246 us
  matrix products: 322 us -> 81.5 us
  blocking collectives: 69.1 us -> 10.3 us
  local copies, waits for them, and re-layouts: 58.4 us -> 22.1 us
  other arithmetic: 41 us -> 16.6 us
  between operations: 16.1 us -> 2.23 us
    reduce_scatter x7 -> x0, waiting for transfers between devices: 292 us -> none  [the longest x1 79.1 us: body(): lax.psum_scatter(up_grad, 'dp', scatter_dimension=0, tiled=True)]
    pallas_call x0 -> x4, Pallas kernels: none -> 246 us  [the longest x1 112 us: scatter_gradients(): pl.pallas_call(functools.partial(scatter_kernel, subs, count), out_shape=...]
    dot_general x37 -> x16, matrix products: 322 us -> 81.5 us  [the longest x1 17.7 us: body(): pre = jnp.dot(hidden_low, w_up, preferred_element_type=F32) + ffn_bias_full]
    all_gather x8 -> x0, waiting for transfers between devices: 227 us -> none  [the longest x1 40.6 us: fetch_weights(): lax.all_gather(key_value_weight, 'dp', axis=1, tiled=True)]
    unnamed x17 -> x0, waiting for transfers between devices: 88.3 us -> none
    psum x1 -> x0, blocking collectives: 42.7 us -> none  [body(): lax.psum((jnp.stack([gain_one, gain_two]), jnp.stack([shift_one, shift_tw...]
    all_gather x1 -> x2, blocking collectives: 26.4 us -> 10.3 us  [the longest x1 5.62 us: body(): lax.all_gather(attn_bias, 'tensor', axis=1, tiled=True).astype(F32)]
    transpose x2 -> x0, local copies, waits for them, and re-layouts: 11.9 us -> none  [the longest x1 6.6 us: body(): jnp.einsum('ld,mle->mde', tokens_all, d_queries, preferred_element_type=j...]
  transfers between devices with their start and end apart: 16 -> 1, of which waited for: 15 -> 1; matrix products, arithmetic and copies ran while one was open for 8% -> 7% of each run, Pallas kernels for 0% -> 0%
where the time goes in v1:
time: 393 us; the launch traced here: 386 us
  Pallas kernels  246 us (63%)
  matrix products  81.5 us (21%)
  local copies, waits for them, and re-layouts  22.1 us (6%)
  other arithmetic  16.6 us (4%)
  blocking collectives  10.3 us (3%)
  waiting for transfers between devices  5.88 us (1%)
    pallas_call x1, Pallas kernels, scatter_gradients(): pl.pallas_call(functools.partial(scatter_kernel, subs, count), out_shape=...  112 us
    pallas_call x1, Pallas kernels, gather_weights(): pl.pallas_call(functools.partial(gather_kernel, subs, count), out_shape=o...  98.9 us
    pallas_call x1, Pallas kernels, attention_forward(): pl.pallas_call(forward_kernel, grid=(pairs,), out_shape=[jax.ShapeDtypeSt...  19 us
    dot_general x1, matrix products, body(): pre = jnp.dot(hidden_low, w_up, preferred_element_type=F32) + ffn_bias_full  17.7 us
    pallas_call x1, Pallas kernels, attention_backward(): pl.pallas_call(backward_kernel, grid=(pairs,), out_shape=[jax.ShapeDtypeS...  16.1 us
  transfers between devices with their start and end apart: 1, of which 1 were waited for; matrix products, arithmetic and copies ran while one was open for 7% of the time, Pallas kernels for 0%

profile of v1, /device:TPU:0, one launch (start us, length us, event | category | flops | bytes accessed | tf_op | source)
XLA Modules:
  0.0 385.7 jit_solution(10869431892703018645)
XLA Ops:
  0.7 5.6 %all_gather.6 = bf16[5,768]{1,0:T(8,128)(2,1)S(1)} all-gather(bf16[5,384]{1,0:T(8,128)(2,1)} %param.22), channel_id=1, replica_groups=mesh['dp'=16,'tensor'=2] {'tensor'}, dimensions={1}, use_global_device_ids=true | all-gather | bytes 11520 | tf_op jit(solution)/shard_map/all_gather | solution.py:592
  6.9 0.8 convert_reduce_fusion.8
  7.7 1.4 fusion.36
  9.0 0.8 dynamic-slice_compare_fusion
  9.8 98.9 %gather_weights.1 = (bf16[2,4,2,2,48,768]{5,4,3,2,1,0:T(8,128)(2,1)}, bf16[4,4,2,2,48,768]{5,4,3,2,1,0:T(8,128)(2,1)}, bf16[1,4,2,2,48,768]{5,4,3,2,1,0:T(8,128)...) custom-call(bf16[2,48,384]{2,1,0:T(8,128)(2,1)} %refs_0_.1, ...), custom_call_target="tpu_custom_call" | custom-call | tf_op jit(solution)/shard_map/gather_weights/pallas_call | solution.py:200
  108.7 1.9 fusion.42
  111.3 1.0 copy.44.seg_col
  112.3 1.0 copy.45.valid_col
  113.4 1.0 copy.46.ent_col
  114.4 5.1 %add_bitcast_fusion = bf16[4,512,768]{2,1,0:T(8,128)(2,1)S(1)} fusion(f32[4,768]{1,0:T(4,128)S(1)} %slice.101, bf16[4,768,768]{2,1,0:T(8,128)(2,1)} %bitcast.166, bf16[512,768]{1,0:T(8,128)(2,1)S(1)} %copy-done.3), kind=kOutput, calls=%fused_computation.18 | convolution fusion | flops 2419064832 | bytes 8663040 | tf_op jit(solution)/shard_map/ld,mde->mle/dot_general | solution.py:600
  119.6 1.4 fusion.25
  121.5 2.5 convolution_convert_fusion.4.keys
  124.0 2.5 add_convert_fusion.1.values
  126.6 19.0 %attention_forward.1 = (bf16[768,512]{1,0:T(8,128)(2,1)}, bf16[12,1024,512]{2,1,0:T(8,128)(2,1)}) custom-call(bf16[512,768]{1,0:T(8,128)(2,1)} %get-tuple-element.84.qw, bf16[512,768]{1,0:T(8,128)(2,1)} %get-tuple-element.83.qe, bf16[1024,768]{1,0:T(8,128)(2,1)} %convolution_convert_fusion.4.keys, bf16[1024,768]{1,0:T(8,128)(2,1)} %add_convert_fusion.1.values, ...), custom_call_target="tpu_custom_call" | custom-call | tf_op jit(solution)/shard_map/attention_forward/pallas_call | solution.py:469
  145.6 2.6 fusion.41
  148.5 4.7 %all-gather = bf16[2,1,1536]{2,1,0:T(2,128)(2,1)S(1)} all-gather(bf16[1,1,1536]{2,1,0:T(2,128)(2,1)S(1)} %reshape.176), channel_id=1, replica_groups=mesh['dp'=16,'tensor'=2] {'tensor'}, dimensions={0}, use_global_device_ids=true | all-gather | bytes 9216 | tf_op jit(solution)/shard_map/all_gather | solution.py:593
  153.3 17.7 %multiply_convert_fusion = (bf16[512,3072]{1,0:T(8,128)(2,1)S(1)}, f32[512,3072]{1,0:T(8,128)S(1)}, f32[512,3072]{1,0:T(8,128)}) fusion(f32[3072]{0:T(1024)S(1)} %bitcast.161, bf16[768,3072]{1,0:T(8,128)(2,1)S(1)} %bitcast.170, f32[512,768]{1,0:T(8,128)S(1)} %get-tuple-element.82, f32[768]{0:T(1024)S(1)} %get-tuple-element.60, ...), kind=kOutput, calls=%fused_computation.5 | convolution fusion | flops 2521694208 | bytes 22042624 | tf_op jit(solution)/shard_map/dot_general | solution.py:622
  171.1 3.7 fusion.13
  175.2 1.6 fusion.10
  176.8 1.6 fusion.38
  178.6 7.3 %convert_reduce_fusion = (f32[3072]{0:T(1024)S(1)}, bf16[512,3072]{1,0:T(8,128)(2,1)S(1)}) fusion(f32[512,3072]{1,0:T(8,128)S(1)} %get-tuple-element.80, f32[512,3072]{1,0:T(8,128)} %get-tuple-element.100, f32[3072]{0:T(1024)S(1)} %bitcast.162, bf16[512,768]{1,0:T(8,128)(2,1)S(1)} %get-tuple-element.70, bf16[768,3072]{1,0:T(8,128)(2,1)S(1)} %bitcast.175), kind=kOutput, calls=%fused_computation.2 | convolution fusion | flops 2442654720 | bytes 21258240 | tf_op jit(solution)/shard_map/dot_general | solution.py:645
  185.9 3.6 multiply_reduce_fusion
  190.4 0.9 copy-done.17
  191.3 1.7 convolution_convert_fusion.6.dctx
  193.0 16.1 %attention_backward.1 = (bf16[768,512]{1,0:T(8,128)(2,1)}, bf16[768,512]{1,0:T(8,128)(2,1)}, bf16[1024,768]{1,0:T(8,128)(2,1)}, bf16[1024,768]{1,0:T(8,128)(2,1)}) custom-call(bf16[12,1024,512]{2,1,0:T(8,128)(2,1)} %get-tuple-element.38.probs, bf16[512,768]{1,0:T(8,128)(2,1)} %get-tuple-element.84.qw, bf16[512,768]{1,0:T(8,128)(2,1)} %get-tuple-element.83.qe, ...), custom_call_target="tpu_custom_call" | custom-call | tf_op jit(solution)/shard_map/attention_backward/pallas_call | solution.py:528
  209.1 2.8 fusion.16
  211.8 1.2 collective-permute-start
  213.1 7.0 %convolution_convert_fusion.1 = bf16[768,3072]{1,0:T(8,128)(2,1)} fusion(bf16[512,768]{1,0:T(8,128)(2,1)} %copy-done.18, bf16[512,3072]{1,0:T(8,128)(2,1)} %copy-done.31), kind=kOutput, calls=%fused_computation.21 | convolution fusion | flops 2418278400 | bytes 8650752 | tf_op jit(solution)/shard_map/ld,lf->df/dot_general | solution.py:648
  220.4 0.9 copy-done.4
  221.2 5.0 %convolution_convert_fusion.2 = bf16[4,768,768]{1,2,0:T(8,128)(2,1)} fusion(bf16[512,768]{1,0:T(8,128)(2,1)S(1)} %copy-done.4, bf16[1,768,512]{2,1,0:T(8,128)(2,1)S(1)} %get-tuple-element.97, bf16[1,768,512]{2,1,0:T(8,128)(2,1)S(1)} %get-tuple-element.91, bf16[1,768,512]{2,1,0:T(8,128)(2,1)S(1)} %get-tuple-element.98, ...), kind=kOutput, calls=%fused_computation.30 | convolution fusion | flops 2422996992 | bytes 8650752 | tf_op jit(solution)/shard_map/ld,mel->mde/dot_general | solution.py:678
  226.9 3.4 convolution_convert_fusion.5
  230.3 5.1 %convolution_convert_fusion = bf16[768,3072]{1,0:T(8,128)(2,1)} fusion(bf16[512,3072]{1,0:T(8,128)(2,1)S(1)} %copy-done.33, f32[512,768]{1,0:T(8,128)S(1)} %get-tuple-element.82, f32[768]{0:T(1024)S(1)} %get-tuple-element.60, f32[768]{0:T(1024)S(1)} %get-tuple-element.102, f32[512]{0:T(512)S(1)} %fusion.29, f32[512]{0:T(512)S(1)} %broadcast_multiply_fusion.1), kind=kOutput, calls=%fused_computation.20 | convolution fusion | flops 2420244480 | bytes 9447424 | tf_op jit(solution)/shard_map/ld,lf->df/dot_general | solution.py:649
  235.5 6.3 %fusion.35 = f32[512,768,1]{1,0,2:T(8,128)} fusion(bf16[4,768,768]{2,1,0:T(8,128)(2,1)} %bitcast.167, bf16[1,768,512]{2,1,0:T(8,128)(2,1)S(1)} %copy-done.11, bf16[1,768,512]{2,1,0:T(8,128)(2,1)S(1)} %copy-done.9, bf16[1,768,512]{2,1,0:T(8,128)(2,1)S(1)} %copy-done.13, bf16[1,768,512]{2,1,0:T(8,128)(2,1)S(1)} %copy-done.7), kind=kOutput, calls=%fused_computation.118 | convolution fusion | flops 2420637696 | bytes 9437184 | tf_op jit(solution)/shard_map/mel,mde->ld/dot_general | solution.py:687
  241.8 5.9 %collective-permute-done = bf16[2,512,768]{2,1,0:T(8,128)(2,1)} collective-permute-done((bf16[2,512,768]{2,1,0:T(8,128)(2,1)}, bf16[2,512,768]{2,1,0:T(8,128)(2,1)}, u32[]{:S(2)}, u32[]{:S(2)}) %collective-permute-start) | collective-permute-done | bytes 1572896 | tf_op jit(solution)/shard_map/ppermute | solution.py:665
  247.7 1.9 fusion.6
  249.6 2.8 convolution_convert_fusion.3
  252.6 3.3 concatenate.8
  256.5 112.1 %scatter_gradients.1 = (f32[1,48,1536]{2,1,0:T(8,128)}, f32[1,48,1536]{2,1,0:T(8,128)}, f32[1,48,384]{2,1,0:T(8,128)}, f32[4,48,384]{2,1,0:T(8,128)}, f32[2,48,384]{2,1,0:T(8,128)}, /*index=5*/f32[96,128]{1,0:T(8,128)}) custom-call(bf16[1,4,2,2,48,3072]{5,4,3,2,1,0:T(8,128)(2,1)} %bitcast.141, bf16[1,4,2,2,48,3072]{5,4,3,2,1,0:T(8,128)(2,1)} %bitcast.143, ...), custom_call_target="tpu_custom_call" | custom-call | tf_op jit(solution)/shard_map/scatter_gradients/pallas_call | solution.py:405
  368.6 0.7 slice.95
  369.3 0.8 fusion.43
  370.1 0.7 slice_bitcast_fusion.4
  370.9 1.3 slice.109
  372.8 1.2 fusion.31
  375.8 4.8 %bitcast_add_fusion = f32[512,768]{1,0:T(8,128)} fusion(f32[512,768,1]{1,0,2:T(8,128)} %fusion.35, bf16[2,512,768]{2,1,0:T(8,128)(2,1)S(1)} %fusion.6, bf16[2,768,768]{2,1,0:T(8,128)(2,1)} %bitcast.145, f32[512,768]{1,0:T(8,128)S(1)} %get-tuple-element.74, f32[512]{0:T(512)S(1)} %negate_multiply_fusion.1), kind=kOutput, calls=%fused_computation.62 | convolution fusion | flops 1209139200 | bytes 8652800 | tf_op jit(solution)/shard_map/mle,mde->ld/dot_general | solution.py:688
  381.2 0.7 dynamic_slice.28
  381.8 0.7 copy.59
  383.9 0.7 copy.62
  384.6 0.7 copy.63
  (111 shorter events, 9.0 us)
Async XLA Ops:
  0.6 110.0 %copy-start.27 = (s32[1024]{0:T(1024)S(1)}, s32[1024]{0:T(1024)}, u32[]{:S(2)}) copy-start(s32[1024]{0:T(1024)} %param.17) | copy-start | bytes 12292
  9.8 102.5 %copy-start.28 = (s32[1024]{0:T(1024)S(1)}, s32[1024]{0:T(1024)}, u32[]{:S(2)}) copy-start(s32[1024]{0:T(1024)} %param.19) | copy-start | bytes 12292
  108.7 4.7 %copy-start.24 = (s32[1024]{0:T(1024)S(1)}, s32[1024]{0:T(1024)}, u32[]{:S(2)}) copy-start(s32[1024]{0:T(1024)} %param.18) | copy-start | bytes 12292
  108.7 5.7 %copy-start.3 = (bf16[512,768]{1,0:T(8,128)(2,1)S(1)}, bf16[512,768]{1,0:T(8,128)(2,1)}, u32[]{:S(2)}) copy-start(bf16[512,768]{1,0:T(8,128)(2,1)} %refs_5_.1) | copy-start | bytes 2359300
  119.6 1.9 copy-start.30
  126.6 26.8 %slice-start = ((s8[4718592]{0:T(1024)(128)(4,1)}), s8[524288]{0:T(1024)(128)(4,1)S(1)}, s32[]{:S(2)}) async-start(s8[4718592]{0:T(1024)(128)(4,1)} %bitcast.168), calls=%async_computation | async-start | bytes 1048576
  145.6 3.0 copy-start.29
  145.6 7.7 %copy-start.25 = (bf16[2,768]{1,0:T(2,128)(2,1)S(1)}, bf16[2,768]{1,0:T(2,128)(2,1)}, u32[]{:S(2)}) copy-start(bf16[2,768]{1,0:T(2,128)(2,1)} %param.26) | copy-start | bytes 9220
  145.6 7.7 %copy-start.26 = (bf16[2,768]{1,0:T(2,128)(2,1)S(1)}, bf16[2,768]{1,0:T(2,128)(2,1)}, u32[]{:S(2)}) copy-start(bf16[2,768]{1,0:T(2,128)(2,1)} %param.25) | copy-start | bytes 9220
  145.6 7.7 %slice-start.1 = ((s8[4718592]{0:T(1024)(128)(4,1)}), s8[4194304]{0:T(1024)(128)(4,1)S(1)}, s32[]{:S(2)}) async-start(s8[4718592]{0:T(1024)(128)(4,1)} %bitcast.168), calls=%async_computation.1 | async-start | bytes 8388608
  145.6 25.5 %slice-start.2 = ((s8[4718592]{0:T(1024)(128)(4,1)}), s8[4194304]{0:T(1024)(128)(4,1)S(1)}, s32[]{:S(2)}) async-start(s8[4718592]{0:T(1024)(128)(4,1)} %bitcast.172), calls=%async_computation.2 | async-start | bytes 8388608
  153.3 17.8 %slice-start.3 = ((s8[4718592]{0:T(1024)(128)(4,1)}), s8[524288]{0:T(1024)(128)(4,1)S(1)}, s32[]{:S(2)}) async-start(s8[4718592]{0:T(1024)(128)(4,1)} %bitcast.172), calls=%async_computation.3 | async-start | bytes 1048576
  171.1 3.8 copy-start.31
  171.1 4.1 %copy-start.2 = (bf16[512,768]{1,0:T(8,128)(2,1)S(1)}, bf16[512,768]{1,0:T(8,128)(2,1)}, u32[]{:S(2)}) copy-start(bf16[512,768]{1,0:T(8,128)(2,1)} %param.16) | copy-start | bytes 2359300
  178.6 7.3 %copy-start.18 = (bf16[512,768]{1,0:T(8,128)(2,1)}, bf16[512,768]{1,0:T(8,128)(2,1)S(1)}, u32[]{:S(2)}) copy-start(bf16[512,768]{1,0:T(8,128)(2,1)S(1)} %get-tuple-element.70) | copy-start | bytes 2359300
  185.9 3.6 copy-start.32
  189.5 1.8 copy-start.14
  190.4 0.9 copy-start.17
  211.8 35.8 %collective-permute-start = (bf16[2,512,768]{2,1,0:T(8,128)(2,1)}, bf16[2,512,768]{2,1,0:T(8,128)(2,1)}, u32[]{:S(2)}, u32[]{:S(2)}) collective-permute-start(bf16[2,512,768]{2,1,0:T(8,128)(2,1)} %fusion.16), channel_id=1, source_target_pairs={{0,1},{1,0},{2,3},{3,2},{4,5},{5,4},{6,7},{7,6},{8,9},{9,8},{10,11... | collective-permute-start | bytes 4718600 | tf_op jit(solution)/shard_map/ppermute | solution.py:665
  213.1 7.0 %copy-start.15 = (bf16[768,512]{1,0:T(8,128)(2,1)S(1)}, bf16[768,512]{1,0:T(8,128)(2,1)}, u32[]{:S(2)}) copy-start(bf16[768,512]{1,0:T(8,128)(2,1)} %get-tuple-element.39) | copy-start | bytes 2359300
  213.1 7.0 %copy-start.16 = (bf16[768,512]{1,0:T(8,128)(2,1)S(1)}, bf16[768,512]{1,0:T(8,128)(2,1)}, u32[]{:S(2)}) copy-start(bf16[768,512]{1,0:T(8,128)(2,1)} %get-tuple-element.40) | copy-start | bytes 2359300
  220.1 1.1 copy-start.4
  220.3 6.0 %copy-start.6 = (bf16[1,768,512]{2,1,0:T(8,128)(2,1)}, bf16[1,768,512]{2,1,0:T(8,128)(2,1)S(1)}, u32[]{:S(2)}) copy-start(bf16[1,768,512]{2,1,0:T(8,128)(2,1)S(1)} %get-tuple-element.90) | copy-start | bytes 2359300
  220.3 5.9 %copy-start.8 = (bf16[1,768,512]{2,1,0:T(8,128)(2,1)}, bf16[1,768,512]{2,1,0:T(8,128)(2,1)S(1)}, u32[]{:S(2)}) copy-start(bf16[1,768,512]{2,1,0:T(8,128)(2,1)S(1)} %get-tuple-element.91) | copy-start | bytes 2359300
  220.3 5.9 %copy-start.10 = (bf16[1,768,512]{2,1,0:T(8,128)(2,1)}, bf16[1,768,512]{2,1,0:T(8,128)(2,1)S(1)}, u32[]{:S(2)}) copy-start(bf16[1,768,512]{2,1,0:T(8,128)(2,1)S(1)} %get-tuple-element.97) | copy-start | bytes 2359300
  220.4 5.9 %copy-start.12 = (bf16[1,768,512]{2,1,0:T(8,128)(2,1)}, bf16[1,768,512]{2,1,0:T(8,128)(2,1)S(1)}, u32[]{:S(2)}) copy-start(bf16[1,768,512]{2,1,0:T(8,128)(2,1)S(1)} %get-tuple-element.98) | copy-start | bytes 2359300
  226.9 3.4 copy-start.33
  230.3 5.2 %copy-start.7 = (bf16[1,768,512]{2,1,0:T(8,128)(2,1)S(1)}, bf16[1,768,512]{2,1,0:T(8,128)(2,1)}, u32[]{:S(2)}) copy-start(bf16[1,768,512]{2,1,0:T(8,128)(2,1)} %copy-done.6) | copy-start | bytes 2359300
  230.3 5.2 %copy-start.9 = (bf16[1,768,512]{2,1,0:T(8,128)(2,1)S(1)}, bf16[1,768,512]{2,1,0:T(8,128)(2,1)}, u32[]{:S(2)}) copy-start(bf16[1,768,512]{2,1,0:T(8,128)(2,1)} %copy-done.8) | copy-start | bytes 2359300
  230.3 5.2 %copy-start.11 = (bf16[1,768,512]{2,1,0:T(8,128)(2,1)S(1)}, bf16[1,768,512]{2,1,0:T(8,128)(2,1)}, u32[]{:S(2)}) copy-start(bf16[1,768,512]{2,1,0:T(8,128)(2,1)} %copy-done.10) | copy-start | bytes 2359300
  230.3 5.2 %copy-start.13 = (bf16[1,768,512]{2,1,0:T(8,128)(2,1)S(1)}, bf16[1,768,512]{2,1,0:T(8,128)(2,1)}, u32[]{:S(2)}) copy-start(bf16[1,768,512]{2,1,0:T(8,128)(2,1)} %copy-done.12) | copy-start | bytes 2359300
  235.5 12.2 %copy-start = (bf16[1024,768]{1,0:T(8,128)(2,1)S(1)}, bf16[1024,768]{1,0:T(8,128)(2,1)}, u32[]{:S(2)}) copy-start(bf16[1024,768]{1,0:T(8,128)(2,1)} %get-tuple-element.41) | copy-start | bytes 4718596
  235.5 12.2 %copy-start.1 = (bf16[1024,768]{1,0:T(8,128)(2,1)S(1)}, bf16[1024,768]{1,0:T(8,128)(2,1)}, u32[]{:S(2)}) copy-start(bf16[1024,768]{1,0:T(8,128)(2,1)} %get-tuple-element.42) | copy-start | bytes 4718596
  241.8 7.7 %copy-start.5 = (bf16[512,768]{1,0:T(8,128)(2,1)S(1)}, bf16[512,768]{1,0:T(8,128)(2,1)}, u32[]{:S(2)}) copy-start(bf16[512,768]{1,0:T(8,128)(2,1)} %refs_5_.1) | copy-start | bytes 2359300
  375.8 6.1 %copy-start.21 = (f32[4,48,384]{2,1,0:T(8,128)S(1)}, f32[4,48,384]{2,1,0:T(8,128)}, u32[]{:S(2)}) copy-start(f32[4,48,384]{2,1,0:T(8,128)} %get-tuple-element.120) | copy-start | bytes 884740
  375.8 6.8 %copy-start.22 = (f32[2,48,384]{2,1,0:T(8,128)S(1)}, f32[2,48,384]{2,1,0:T(8,128)}, u32[]{:S(2)}) copy-start(f32[2,48,384]{2,1,0:T(8,128)} %get-tuple-element.121) | copy-start | bytes 442372
  375.8 7.4 %copy-start.23 = (f32[1,48,384]{2,1,0:T(8,128)S(1)}, f32[1,48,384]{2,1,0:T(8,128)}, u32[]{:S(2)}) copy-start(f32[1,48,384]{2,1,0:T(8,128)} %get-tuple-element.46) | copy-start | bytes 221188
  375.8 8.1 %copy-start.20 = (f32[1,48,1536]{2,1,0:T(8,128)S(1)}, f32[1,48,1536]{2,1,0:T(8,128)}, u32[]{:S(2)}) copy-start(f32[1,48,1536]{2,1,0:T(8,128)} %get-tuple-element.47) | copy-start | bytes 884740
  375.8 8.8 %copy-start.19 = (f32[1,48,1536]{2,1,0:T(8,128)S(1)}, f32[1,48,1536]{2,1,0:T(8,128)}, u32[]{:S(2)}) copy-start(f32[1,48,1536]{2,1,0:T(8,128)} %get-tuple-element.48) | copy-start | bytes 884740

commit v2 on v1

--- a/solution.py
+++ b/solution.py
@@ -38,6 +38,7 @@
         self.x = (block // 2) % 2
         self.c = block % 2
         self.y = lax.axis_index("tensor")
+        self.moved = self.y != self.c
         self.x1 = jnp.where(self.c == 0, 1 - self.x, self.x)
         self.y1 = jnp.where(self.c == 0, self.y, 1 - self.y)
         self.x2 = jnp.where(self.c == 0, self.x, 1 - self.x)
@@ -61,6 +62,12 @@
 
     def sibling(self):
         return self.device(c=1 - self.c)
+
+    def across(self):
+        return self.device(y=1 - self.y)
+
+    def transposed(self):
+        return self.device(c=1 - self.c, y=1 - self.y)
 
     def pieces(self):
         return (
@@ -74,7 +81,7 @@
 def entry_barrier(place):
     barrier = pltpu.get_barrier_semaphore()
     peers = [place.z_peer(step) for step in (1, 2, 3)]
-    peers += [place.device(x=1 - place.x), place.device(y=1 - place.y), place.sibling()]
+    peers += [place.device(x=1 - place.x), place.across(), place.sibling(), place.transposed()]
     for peer in peers:
         pl.semaphore_signal(barrier, inc=1, device_id=peer, device_id_type=MESH)
     pl.semaphore_wait(barrier, len(peers))
@@ -167,54 +174,117 @@
     return order
 
 
+class Share:
+    def __init__(self, source, pair, index, peer, sems):
+        self.kept = pltpu.make_async_copy(source, pair.at[index], sems.at[2])
+        self.sent = remote(source, pair.at[index], sems.at[0], sems.at[1], peer)
+
+    def start(self):
+        self.kept.start()
+        self.sent.start()
+
+    def finish(self):
+        self.kept.wait()
+        self.sent.wait()
+
+
+class Rows:
+    def __init__(self, place, rows, both, sems):
+        p = place
+        half = both.at[p.c]
+        self.moved = p.moved
+        self.kept = pltpu.make_async_copy(rows, half, sems.at[4])
+        self.swap = remote(rows, both.at[p.y], sems.at[0], sems.at[1], p.transposed())
+        self.swapped = remote(half, half, sems.at[0], sems.at[1], p.transposed())
+        self.share = remote(rows, half, sems.at[2], sems.at[3], p.sibling())
+        self.relay = remote(half, half, sems.at[2], sems.at[3], p.sibling())
+        other = both.at[1 - p.c]
+        self.other = remote(other, other, sems.at[2], sems.at[3], p.sibling())
+
+    def start(self):
+        @pl.when(self.moved)
+        def _():
+            self.swap.start()
+
+        @pl.when(jnp.logical_not(self.moved))
+        def _():
+            self.kept.start()
+            self.share.start()
+
+    def forward(self):
+        @pl.when(self.moved)
+        def _():
+            self.swapped.wait_recv()
+            self.relay.start()
+
+    def finish(self):
+        @pl.when(self.moved)
+        def _():
+            self.swap.wait_send()
+            self.relay.wait_send()
+
+        @pl.when(jnp.logical_not(self.moved))
+        def _():
+            self.kept.wait()
+            self.share.wait_send()
+
+        self.other.wait_recv()
+
+
 def gather_kernel(subs, count, *refs):
-    shards, rows = refs[:count], refs[count]
-    fulls, both = refs[count + 1 : 2 * count + 1], refs[2 * count + 1]
-    send, recv, local, row_sems = refs[2 * count + 2 :]
+    shards, (rows, bias, facts) = refs[:count], refs[count : count + 3]
+    fulls, (both, biases, pair_facts) = refs[count + 3 : 2 * count + 3], refs[2 * count + 3 : 2 * count + 6]
+    send, recv, local, row_sems, share_sems = refs[2 * count + 6 :]
     place = Place(subs)
     entry_barrier(place)
-    kept = pltpu.make_async_copy(rows, both.at[place.y], row_sems.at[0])
-    kept.start()
-    across = remote(
-        rows, both.at[place.y], row_sems.at[1], row_sems.at[2], place.device(y=1 - place.y)
-    )
-    across.start()
+    tokens = Rows(place, rows, both, row_sems)
+    shares = [
+        Share(facts, pair_facts, place.c, place.sibling(), share_sems.at[0]),
+        Share(bias, biases, place.y, place.across(), share_sems.at[1]),
+    ]
+    tokens.start()
+    for share in shares:
+        share.start()
     movers = [
         Gather(place, shards[i], fulls[i], send.at[i], recv.at[i], local.at[i]) for i in range(count)
     ]
     for mover in movers:
         mover.stage1()
-    for step in wavefront(movers):
+    for index, step in enumerate(wavefront(movers)):
         if step.__func__ is not Gather.stage1:
             step()
-    kept.wait()
-    across.wait()
-
-
-def gather_weights(subs, shards, rows):
+        if index == count:
+            tokens.forward()
+    tokens.finish()
+    for share in shares:
+        share.finish()
+
+
+def gather_weights(subs, shards, rows, bias, facts):
     count = len(shards)
     outs = [
         jax.ShapeDtypeStruct((s.shape[0], 4, 2, 2, s.shape[1], 2 * s.shape[2]), BF16) for s in shards
     ]
-    outs.append(jax.ShapeDtypeStruct((2,) + rows.shape, BF16))
+    outs += [jax.ShapeDtypeStruct((2,) + a.shape, a.dtype) for a in (rows, bias, facts)]
     results = pl.pallas_call(
         functools.partial(gather_kernel, subs, count),
         out_shape=outs,
-        in_specs=[pl.BlockSpec(memory_space=pltpu.VMEM)] * (count + 1),
-        out_specs=[pl.BlockSpec(memory_space=pl.ANY)] * (count + 1),
+        in_specs=[pl.BlockSpec(memory_space=pltpu.VMEM)] * (count + 3),
+        out_specs=[pl.BlockSpec(memory_space=pl.ANY)] * (count + 3),
         scratch_shapes=[
             pltpu.SemaphoreType.DMA((count, 10)),
             pltpu.SemaphoreType.DMA((count, 10)),
             pltpu.SemaphoreType.DMA((count,)),
-            pltpu.SemaphoreType.DMA((3,)),
+            pltpu.SemaphoreType.DMA((5,)),
+            pltpu.SemaphoreType.DMA((2, 3)),
         ],
         compiler_params=pltpu.CompilerParams(
             collective_id=0, has_side_effects=True, vmem_limit_bytes=VMEM_LIMIT
         ),
         name="gather_weights",
-    )(*shards, rows)
+    )(*shards, rows, bias, facts)
     fulls = [r.reshape(r.shape[0], GRID * r.shape[4], r.shape[5]) for r in results[:count]]
-    return fulls, results[count]
+    return fulls, results[count:]
 
 
 class Scatter:
@@ -572,7 +642,22 @@
     length = segment.shape[0]
     rank = lax.axis_index("tensor")
     subs = lax.axis_size("dp") // GRID
-    start = rank * rows
+    core = (lax.axis_index("dp") // subs) % 2
+    moved = rank != core
+    start = core * rows
+    pairs = lax.axis_size("tensor")
+    trades = []
+    for d in range(lax.axis_size("dp")):
+        other = d + subs if (d // subs) % 2 == 0 else d - subs
+        y = 1 - (d // subs) % 2
+        trades.append((d * pairs + y, other * pairs + 1 - y))
+    siblings = [
+        (d, d + subs if (d // subs) % 2 == 0 else d - subs) for d in range(lax.axis_size("dp"))
+    ]
+
+    def trade(own):
+        got = lax.ppermute(own, ("dp", "tensor"), trades)
+        return jnp.where(moved, got, own)
 
     shards = [
         query_weight,
@@ -587,11 +672,24 @@
             lax.all_gather(s, "dp", axis=1, tiled=True, axis_index_groups=groups) for s in shards
         ]
     shards = [shards[1], shards[0]] + shards[2:]
-    (w_kv, w_q, w_out_t, w_up, w_down_t), both = gather_weights(subs, shards, layer_input)
+    units = pairs * ffn_bias.shape[0]
+    cols = attn_bias.shape[1]
+    bias_rows = jnp.concatenate([attn_bias, ffn_bias.reshape(-1, cols)]).astype(F32)
+    used = bias_rows.shape[0]
+    bias_rows = jnp.pad(bias_rows, ((0, -used % 16), (0, 0)))
+    facts = jnp.pad(jnp.stack([segment, entity, valid_mask]), ((0, 5), (0, 0)))
+    (w_kv, w_q, w_out_t, w_up, w_down_t), (both, biases, pair_facts) = gather_weights(
+        subs, shards, layer_input, bias_rows, facts
+    )
+    grad_out, both = lax.optimization_barrier((grad_out, both))
+    grad_out = trade(grad_out)
     w_out_t, w_up, w_down_t = w_out_t[0], w_up[0], w_down_t[0]
-    bias_full = lax.all_gather(attn_bias, "tensor", axis=1, tiled=True).astype(F32)
-    ffn_bias_full = lax.all_gather(ffn_bias, "tensor", axis=0, tiled=True).astype(F32)
+    bias_full = jnp.moveaxis(biases[:, :5], 0, 1).reshape(5, width)
+    ffn_bias_full = biases[:, 5:used].reshape(units)
+    facts = lax.dynamic_index_in_dim(pair_facts, rank, 0, keepdims=False)
+    segment, entity, valid_mask = facts[0], facts[1], facts[2]
     tokens = both.reshape(length, width)
+    layer_input = lax.dynamic_index_in_dim(both, core, 0, keepdims=False)
 
     ent_own = lax.dynamic_slice_in_dim(entity, start, rows)
     valid_own = lax.dynamic_slice_in_dim(valid_mask, start, rows).astype(F32)[:, None]
@@ -628,7 +726,7 @@
     result, ln_two_pull = jax.vjp(
         layer_norm, resid_two, ln_gain[1].astype(F32), ln_bias[1].astype(F32)
     )
-    output = result.astype(BF16)
+    output = trade(result.astype(BF16))
     stats = jnp.stack(
         [
             jnp.sum(valid_own * resid_one * resid_one),
@@ -658,11 +756,10 @@
     d_word_t, d_ent_t, d_keys_all, d_values_all = attention_backward(
         probs, query_word, query_ent, keys, values, context_t, d_context_t, ent_col, ent_row
     )
-    pairs = lax.axis_size("tensor")
     stacked = jnp.stack([d_keys_all, d_values_all]).reshape(2, 2, rows, width)
-    mine = lax.dynamic_index_in_dim(stacked, rank, 1, keepdims=False)
-    theirs = lax.dynamic_index_in_dim(stacked, 1 - rank, 1, keepdims=False)
-    swapped = lax.ppermute(theirs, "tensor", [(i, pairs - 1 - i) for i in range(pairs)])
+    mine = lax.dynamic_index_in_dim(stacked, core, 1, keepdims=False)
+    theirs = lax.dynamic_index_in_dim(stacked, 1 - core, 1, keepdims=False)
+    swapped = lax.ppermute(theirs, "dp", siblings)
     d_kv = (mine.astype(F32) + swapped.astype(F32)).astype(BF16)
 
     ent_lane = (ent_own == 1)[None, :]
@@ -687,6 +784,8 @@
         + jnp.einsum("mel,mde->ld", d_queries_t, w_q, preferred_element_type=F32)
         + jnp.einsum("mle,mde->ld", d_kv, w_kv, preferred_element_type=F32)
     )
+    returned = lax.ppermute(input_grad.astype(BF16), ("dp", "tensor"), trades)
+    input_grad = jnp.where(moved, returned.astype(F32), input_grad)
 
     pieces = [
         gain_one,
@@ -717,10 +816,8 @@
     shifts = flat[2 * width : 4 * width].reshape(2, width)
     out_biases = flat[4 * width : 6 * width].reshape(2, width)
     attn_biases = flat[6 * width : 11 * width].reshape(5, width)
-    units = ffn_bias_full.shape[0]
     ffn_biases = flat[11 * width : 11 * width + units]
     stat_sum = flat[11 * width + units : 11 * width + units + 5]
-    cols = attn_bias.shape[1]
     half = ffn_bias.shape[0]
     return (
         output,

time: 393 us -> 391 us (level)
  blocking collectives: 10.3 us -> 0 us
  starting transfers between devices: 1.22 us -> 9.18 us
  local copies, waits for them, and re-layouts: 22.1 us -> 28.8 us
  matrix products: 81.5 us -> 75.5 us
  waiting for transfers between devices: 5.88 us -> 0.01 us
  other arithmetic: 16.6 us -> 21.4 us
    all_gather x2 -> x0, blocking collectives: 10.3 us -> none  [the longest x1 5.62 us: body(): lax.all_gather(attn_bias, 'tensor', axis=1, tiled=True).astype(F32)]
    ppermute x1 -> x4, starting transfers between devices: 1.22 us -> 9.18 us  [the longest x1 5.37 us: body(): swapped = lax.ppermute(theirs, 'dp', siblings)]
    ppermute x1 -> x4, waiting for transfers between devices: 5.88 us -> 0.01 us  [the longest x2 0.01 us: trade(): got = lax.ppermute(own, ('dp', 'tensor'), trades)]
  transfers between devices with their start and end apart: 1 -> 4, of which waited for: 1 -> 0; matrix products, arithmetic and copies ran while one was open for 7% -> 22% of each run, Pallas kernels for 0% -> 38%
where the time goes in v2:
time: 391 us; the launch traced here: 385 us
  Pallas kernels  248 us (63%)
  matrix products  75.5 us (19%)
  local copies, waits for them, and re-layouts  28.8 us (7%)
  other arithmetic  21.4 us (5%)
  starting transfers between devices  9.18 us (2%)
    pallas_call x1, Pallas kernels, scatter_gradients(): pl.pallas_call(functools.partial(scatter_kernel, subs, count), out_shape=...  111 us
    pallas_call x1, Pallas kernels, gather_weights(): pl.pallas_call(functools.partial(gather_kernel, subs, count), out_shape=o...  102 us
    dot_general x1, matrix products, body(): pre = jnp.dot(hidden_low, w_up, preferred_element_type=F32) + ffn_bias_full  19.7 us
    pallas_call x1, Pallas kernels, attention_forward(): pl.pallas_call(forward_kernel, grid=(pairs,), out_shape=[jax.ShapeDtypeSt...  19.2 us
    pallas_call x1, Pallas kernels, attention_backward(): pl.pallas_call(backward_kernel, grid=(pairs,), out_shape=[jax.ShapeDtypeS...  16.5 us
  transfers between devices with their start and end apart: 4, of which 0 were waited for; matrix products, arithmetic and copies ran while one was open for 22% of the time, Pallas kernels for 38%

profile of v2, /device:TPU:0, one launch (start us, length us, event | category | flops | bytes accessed | tf_op | source)
XLA Modules:
  0.0 384.9 jit_solution(691773857926198666)
XLA Ops:
  1.3 1.3 fusion.35.refs_6_
  4.0 102.0 %gather_weights.1 = (bf16[2,4,2,2,48,768]{5,4,3,2,1,0:T(8,128)(2,1)}, bf16[4,4,2,2,48,768]{5,4,3,2,1,0:T(8,128)(2,1)}, bf16[1,4,2,2,48,768]{5,4,3,2,1,0:T(8,128)...) custom-call(bf16[2,48,384]{2,1,0:T(8,128)(2,1)} %refs_0_.1, ...), custom_call_target="tpu_custom_call" | custom-call | tf_op jit(solution)/shard_map/gather_weights/pallas_call | solution.py:269
  106.0 1.6 collective-permute-start.1
  107.5 0.7 slice_bitcast_fusion.4
  108.3 1.4 fusion.49
  109.7 0.8 compare_reduce_fusion
  110.5 1.5 fusion.41
  112.0 1.3 fusion.39.seg_row
  113.9 0.8 slice.115
  114.7 0.8 convert_reduce_fusion.8
  115.5 1.8 fusion.55
  117.3 1.1 copy.37.seg_col
  118.4 1.0 copy.38.valid_col
  119.4 1.0 copy.39.ent_col
  120.4 5.2 %add_bitcast_fusion = bf16[4,512,768]{2,1,0:T(8,128)(2,1)S(1)} fusion(f32[4,768]{1,0:T(4,128)S(1)} %bitcast.178, bf16[4,768,768]{2,1,0:T(8,128)(2,1)} %bitcast.185, bf16[2,512,768]{2,1,0:T(8,128)(2,1)} %get-tuple-element.36, s32[]{:T(128)S(6)} %select_n.73), kind=kOutput, calls=%fused_computation.18 | convolution fusion | flops 2419064832 | bytes 8663044 | tf_op jit(solution)/shard_map/ld,mde->mle/dot_general | solution.py:698
  125.6 1.4 fusion.25
  127.5 2.5 convolution_convert_fusion.4.keys
  130.1 2.6 add_convert_fusion.1.values
  132.6 19.2 %attention_forward.1 = (bf16[768,512]{1,0:T(8,128)(2,1)}, bf16[12,1024,512]{2,1,0:T(8,128)(2,1)}) custom-call(bf16[512,768]{1,0:T(8,128)(2,1)} %get-tuple-element.93.qw, bf16[512,768]{1,0:T(8,128)(2,1)} %get-tuple-element.92.qe, bf16[1024,768]{1,0:T(8,128)(2,1)} %convolution_convert_fusion.4.keys, bf16[1024,768]{1,0:T(8,128)(2,1)} %add_convert_fusion.1.values, ...), custom_call_target="tpu_custom_call" | custom-call | tf_op jit(solution)/shard_map/attention_forward/pallas_call | solution.py:539
  151.9 3.4 fusion.54
  155.7 19.7 %multiply_convert_fusion = (bf16[512,3072]{1,0:T(8,128)(2,1)S(1)}, f32[512,3072]{1,0:T(8,128)}, f32[512,3072]{1,0:T(8,128)}) fusion(f32[3072]{0:T(1024)S(1)} %add.195, bf16[768,3072]{1,0:T(8,128)(2,1)} %bitcast.189, f32[512,768]{1,0:T(8,128)S(1)} %get-tuple-element.91, f32[768]{0:T(1024)S(1)} %get-tuple-element.68, f32[768]{0:T(1024)S(1)} %get-tuple-element.117, ...), kind=kOutput, calls=%fused_computation.5 | convolution fusion | flops 2521694208 | bytes 22042624 | tf_op jit(solution)/shard_map/dot_general | solution.py:720
  175.4 1.6 copy-done.18
  177.1 6.0 %fusion.13 = (f32[]{:T(128)}, f32[]{:T(128)}, f32[512]{0:T(512)S(1)}, f32[512,768]{1,0:T(8,128)S(1)}) fusion(f32[512]{0:T(512)S(1)} %bitcast.179, f32[768]{0:T(1024)S(1)} %get-tuple-element.69, f32[512,768]{1,0:T(8,128)S(1)} %copy-done.4, f32[768]{0:T(1024)S(1)} %get-tuple-element.68, f32[768]{0:T(1024)S(1)} %get-tuple-element.117, f32[512]{0:T(512)S(1)} %fusion.42, ...), kind=kOutput, calls=%fused_computation.48 | convolution fusion | flops 2421030400 | bytes 12600328 | tf_op jit(solution)/shard_map/lf,df->ld/dot_general | solution.py:723
  183.5 3.1 fusion.10
  186.6 1.6 fusion.51
  188.7 4.3 %convolution_convert_fusion.1 = bf16[768,3072]{1,0:T(8,128)(2,1)} fusion(bf16[512,768]{1,0:T(8,128)(2,1)S(1)} %get-tuple-element.78, bf16[512,3072]{1,0:T(8,128)(2,1)S(1)} %copy-done.19), kind=kOutput, calls=%fused_computation.21 | convolution fusion | flops 2418278400 | bytes 8650752 | tf_op jit(solution)/shard_map/ld,lf->df/dot_general | solution.py:746
  193.1 6.9 %convert_reduce_fusion = (f32[3072]{0:T(1024)S(1)}, bf16[512,3072]{1,0:T(8,128)(2,1)S(1)}) fusion(f32[512,3072]{1,0:T(8,128)S(1)} %bitcast.198, f32[512,3072]{1,0:T(8,128)} %get-tuple-element.113, f32[3072]{0:T(1024)S(1)} %add.195, bf16[512,768]{1,0:T(8,128)(2,1)S(1)} %get-tuple-element.78, bf16[768,3072]{1,0:T(8,128)(2,1)S(1)} %bitcast.196), kind=kOutput, calls=%fused_computation.2 | convolution fusion | flops 2442654720 | bytes 21258240 | tf_op jit(solution)/shard_map/dot_general | solution.py:743
  200.0 3.6 multiply_reduce_fusion
  203.6 4.8 %convolution_convert_fusion = bf16[768,3072]{1,0:T(8,128)(2,1)} fusion(bf16[512,3072]{1,0:T(8,128)(2,1)S(1)} %get-tuple-element.76, f32[512,768]{1,0:T(8,128)S(1)} %get-tuple-element.91, f32[768]{0:T(1024)S(1)} %get-tuple-element.68, f32[768]{0:T(1024)S(1)} %get-tuple-element.117, f32[512]{0:T(512)S(1)} %fusion.42, f32[512]{0:T(512)S(1)} %broadcast_multiply_fusion.1), kind=kOutput, calls=%fused_computation.20 | convolution fusion | flops 2420244480 | bytes 9447424 | tf_op jit(solution)/shard_map/ld,lf->df/dot_general | solution.py:747
  208.4 1.6 collective-permute-start
  210.8 1.0 copy-done.6
  211.9 1.7 convolution_convert_fusion.6.dctx
  213.6 16.5 %attention_backward.1 = (bf16[768,512]{1,0:T(8,128)(2,1)}, bf16[768,512]{1,0:T(8,128)(2,1)}, bf16[1024,768]{1,0:T(8,128)(2,1)}, bf16[1024,768]{1,0:T(8,128)(2,1)}) custom-call(bf16[12,1024,512]{2,1,0:T(8,128)(2,1)} %get-tuple-element.46.probs, bf16[512,768]{1,0:T(8,128)(2,1)} %get-tuple-element.93.qw, bf16[512,768]{1,0:T(8,128)(2,1)} %get-tuple-element.92.qe, ...), custom_call_target="tpu_custom_call" | custom-call | tf_op jit(solution)/shard_map/attention_backward/pallas_call | solution.py:598
  230.2 1.7 fusion.16
  231.8 5.4 %collective-permute-start.2 = (bf16[2,512,768]{2,1,0:T(8,128)(2,1)S(1)}, bf16[2,512,768]{2,1,0:T(8,128)(2,1)S(1)}, u32[]{:S(2)}, u32[]{:S(2)}) collective-permute-start(bf16[2,512,768]{2,1,0:T(8,128)(2,1)S(1)} %fusion.16), channel_id=1, source_target_pairs={{0,2},{2,0},{4,6},{6,4},{8,10},{10,8},{12,14},{14,12},{16,18},{18,... | collective-permute-start | bytes 4718600 | tf_op jit(solution)/shard_map/ppermute | solution.py:762
  238.6 1.8 convolution_convert_fusion.5
  240.4 5.0 %convolution_convert_fusion.2 = bf16[4,768,768]{1,2,0:T(8,128)(2,1)} fusion(bf16[2,512,768]{2,1,0:T(8,128)(2,1)S(1)} %copy-done.10, s32[]{:T(128)S(6)} %select_n.73, bf16[1,768,512]{2,1,0:T(8,128)(2,1)S(1)} %get-tuple-element.110, bf16[1,768,512]{2,1,0:T(8,128)(2,1)S(1)} %get-tuple-element.100, bf16[1,768,512]{2,1,0:T(8,128)(2,1)S(1)} %get-tuple-element.111, ...), kind=kOutput, calls=%fused_computation.30 | convolution fusion | flops 2422996992 | bytes 8650756 | tf_op jit(solution)/shard_map/ld,mel->mde/dot_general | solution.py:775
  245.4 2.7 fusion.48
  248.1 2.2 broadcast_select_fusion.1
  250.8 2.9 convolution_convert_fusion.3
  253.9 2.3 fusion.57
  257.0 3.3 concatenate.12
  260.9 110.5 %scatter_gradients.1 = (f32[1,48,1536]{2,1,0:T(8,128)}, f32[1,48,1536]{2,1,0:T(8,128)}, f32[1,48,384]{2,1,0:T(8,128)}, f32[4,48,384]{2,1,0:T(8,128)}, f32[2,48,384]{2,1,0:T(8,128)}, /*index=5*/f32[96,128]{1,0:T(8,128)}) custom-call(bf16[1,4,2,2,48,3072]{5,4,3,2,1,0:T(8,128)(2,1)} %bitcast.158, bf16[1,4,2,2,48,3072]{5,4,3,2,1,0:T(8,128)(2,1)} %bitcast.159, ...), custom_call_target="tpu_custom_call" | custom-call | tf_op jit(solution)/shard_map/scatter_gradients/pallas_call | solution.py:475
  371.5 0.8 slice.123
  372.2 1.3 slice.137
  373.5 0.8 fusion.56
  378.7 1.2 fusion.44
  380.0 1.4 convert_select_fusion
  (105 shorter events, 15.9 us)
Async XLA Ops:
  106.0 77.5 %collective-permute-start.1 = (bf16[512,768]{1,0:T(8,128)(2,1)}, bf16[512,768]{1,0:T(8,128)(2,1)}, u32[]{:S(2)}, u32[]{:S(2)}) collective-permute-start(bf16[512,768]{1,0:T(8,128)(2,1)} %param.16), channel_id=1, source_target_pairs={{1,2},{2,1},{5,6},{6,5},{9,10},{10,9},{13,14},{14,13},{17,18},{18,... | collective-permute-start | bytes 2359304 | tf_op jit(solution)/shard_map/ppermute | solution.py:659
  125.6 1.9 copy-start.9
  132.6 19.2 %copy-start.5 = (bf16[1,4,2,2,48,768]{5,4,3,2,1,0:T(8,128)(2,1)S(1)}, bf16[1,4,2,2,48,768]{5,4,3,2,1,0:T(8,128)(2,1)}, u32[]{:S(2)}) copy-start(bf16[1,4,2,2,48,768]{5,4,3,2,1,0:T(8,128)(2,1)} %get-tuple-element.42) | copy-start | bytes 3538948
  151.9 3.7 copy-start.16
  151.9 3.7 copy-start.17
  155.7 21.4 %copy-start.4 = (f32[512,768]{1,0:T(8,128)S(1)}, f32[512,768]{1,0:T(8,128)}, u32[]{:S(2)}) copy-start(f32[512,768]{1,0:T(8,128)} %get-tuple-element.112) | copy-start | bytes 4718596
  175.4 1.6 copy-start.18
  183.4 9.6 %slice-start.6 = ((s8[6291456]{0:T(1024)(128)(4,1)}), s8[4194304]{0:T(1024)(128)(4,1)S(1)}, s32[]{:S(2)}) async-start(s8[6291456]{0:T(1024)(128)(4,1)} %bitcast.197), calls=%async_computation.6 | async-start | bytes 8388608
  186.5 2.2 copy-start.19
  186.5 6.5 %slice-start.4 = ((s8[4718592]{0:T(1024)(128)(4,1)}), s8[4194304]{0:T(1024)(128)(4,1)S(1)}, s32[]{:S(2)}) async-start(s8[4718592]{0:T(1024)(128)(4,1)} %bitcast.194), calls=%async_computation.4 | async-start | bytes 8388608
  188.7 4.3 %slice-start.5 = ((s8[4718592]{0:T(1024)(128)(4,1)}), s8[524288]{0:T(1024)(128)(4,1)S(1)}, s32[]{:S(2)}) async-start(s8[4718592]{0:T(1024)(128)(4,1)} %bitcast.194), calls=%async_computation.5 | async-start | bytes 1048576
  188.7 4.3 %slice-start.7 = ((s8[6291456]{0:T(1024)(128)(4,1)}), s8[2097152]{0:T(1024)(128)(4,1)S(1)}, s32[]{:S(2)}) async-start(s8[6291456]{0:T(1024)(128)(4,1)} %bitcast.197), calls=%async_computation.7 | async-start | bytes 4194304
  188.7 11.3 %slice-start.2 = ((s8[4718592]{0:T(1024)(128)(4,1)}), s8[4194304]{0:T(1024)(128)(4,1)S(1)}, s32[]{:S(2)}) async-start(s8[4718592]{0:T(1024)(128)(4,1)} %bitcast.190), calls=%async_computation.2 | async-start | bytes 8388608
  193.1 6.9 %slice-start.3 = ((s8[4718592]{0:T(1024)(128)(4,1)}), s8[524288]{0:T(1024)(128)(4,1)S(1)}, s32[]{:S(2)}) async-start(s8[4718592]{0:T(1024)(128)(4,1)} %bitcast.190), calls=%async_computation.3 | async-start | bytes 1048576
  208.4 39.7 %collective-permute-start = (bf16[512,768]{1,0:T(8,128)(2,1)}, bf16[512,768]{1,0:T(8,128)(2,1)}, u32[]{:S(2)}, u32[]{:S(2)}) collective-permute-start(bf16[512,768]{1,0:T(8,128)(2,1)} %get-tuple-element.96), channel_id=1, source_target_pairs={{1,2},{2,1},{5,6},{6,5},{9,10},{10,9},{13,14},{14,13},{17,18},{18,... | collective-permute-start | bytes 2359304 | tf_op jit(solution)/shard_map/ppermute | solution.py:659
  210.6 1.3 copy-start.6
  230.1 7.1 %copy-start.7 = (bf16[768,512]{1,0:T(8,128)(2,1)S(1)}, bf16[768,512]{1,0:T(8,128)(2,1)}, u32[]{:S(2)}) copy-start(bf16[768,512]{1,0:T(8,128)(2,1)} %get-tuple-element.47) | copy-start | bytes 2359300
  230.1 7.1 %copy-start.8 = (bf16[768,512]{1,0:T(8,128)(2,1)S(1)}, bf16[768,512]{1,0:T(8,128)(2,1)}, u32[]{:S(2)}) copy-start(bf16[768,512]{1,0:T(8,128)(2,1)} %get-tuple-element.48) | copy-start | bytes 2359300
  230.2 15.2 %slice-start = ((s8[4718592]{0:T(1024)(128)(4,1)}), s8[4194304]{0:T(1024)(128)(4,1)S(1)}, s32[]{:S(2)}) async-start(s8[4718592]{0:T(1024)(128)(4,1)} %bitcast.186), calls=%async_computation | async-start | bytes 8388608
  231.8 18.5 %collective-permute-start.2 = (bf16[2,512,768]{2,1,0:T(8,128)(2,1)S(1)}, bf16[2,512,768]{2,1,0:T(8,128)(2,1)S(1)}, u32[]{:S(2)}, u32[]{:S(2)}) collective-permute-start(bf16[2,512,768]{2,1,0:T(8,128)(2,1)S(1)} %fusion.16), channel_id=1, source_target_pairs={{0,2},{2,0},{4,6},{6,4},{8,10},{10,8},{12,14},{14,12},{16,18},{18,... | collective-permute-start | bytes 4718600 | tf_op jit(solution)/shard_map/ppermute | solution.py:762
  237.4 1.1 copy-start.2
  238.6 1.8 copy-start.10
  240.4 5.0 %slice-start.1 = ((s8[4718592]{0:T(1024)(128)(4,1)}), s8[524288]{0:T(1024)(128)(4,1)S(1)}, s32[]{:S(2)}) async-start(s8[4718592]{0:T(1024)(128)(4,1)} %bitcast.186), calls=%async_computation.1 | async-start | bytes 1048576
  245.4 4.9 %copy-start.1 = (bf16[1024,768]{1,0:T(8,128)(2,1)S(1)}, bf16[1024,768]{1,0:T(8,128)(2,1)}, u32[]{:S(2)}) copy-start(bf16[1024,768]{1,0:T(8,128)(2,1)} %get-tuple-element.50) | copy-start | bytes 4718596
  248.1 2.3 copy-start
  250.8 3.1 copy-start.3
  256.2 123.7 %collective-permute-start.3 = (bf16[512,768]{1,0:T(8,128)(2,1)}, bf16[512,768]{1,0:T(8,128)(2,1)S(1)}, u32[]{:S(2)}, u32[]{:S(2)}) collective-permute-start(bf16[512,768]{1,0:T(8,128)(2,1)} %get-tuple-element.115), channel_id=1, source_target_pairs={{1,2},{2,1},{5,6},{6,5},{9,10},{10,9},{13,14},{14,13},{17,18},{18,... | collective-permute-start | bytes 2359304 | tf_op jit(solution)/shard_map/ppermute | solution.py:787
  371.4 9.9 %copy-start.13 = (f32[4,48,384]{2,1,0:T(8,128)S(1)}, f32[4,48,384]{2,1,0:T(8,128)}, u32[]{:S(2)}) copy-start(f32[4,48,384]{2,1,0:T(8,128)} %get-tuple-element.135) | copy-start | bytes 884740
  373.5 8.6 %copy-start.14 = (f32[2,48,384]{2,1,0:T(8,128)S(1)}, f32[2,48,384]{2,1,0:T(8,128)}, u32[]{:S(2)}) copy-start(f32[2,48,384]{2,1,0:T(8,128)} %get-tuple-element.136) | copy-start | bytes 442372
  379.9 2.8 copy-start.15
  379.9 3.4 copy-start.12
  379.9 4.1 %copy-start.11 = (f32[1,48,1536]{2,1,0:T(8,128)S(1)}, f32[1,48,1536]{2,1,0:T(8,128)}, u32[]{:S(2)}) copy-start(f32[1,48,1536]{2,1,0:T(8,128)} %get-tuple-element.56) | copy-start | bytes 884740
